TPU v7x, 32 devices: a whole 2x2x4 slice. The times are simulated.
32 devices in a mesh: groups: 2 (over y), ctx: 4 (over z), head: 2 (over x), sub: 2 (over core).
Axes of the slice: x: 2, y: 2, z: 4, core: 2. Of those that a mesh axis runs over, the one named last changes fastest.
Arguments:
- tokens: bfloat16 [8192, 768], P(('groups', 'ctx', 'sub')), parts along dimension 0, may hold values from -6 to 6
- norm_gain: float32 [768], replicated, may hold values from 0.1 to 1.9
- w_qkv: bfloat16 [768, 3, 768], P(None, None, 'head'), may hold values from -0.21875 to 0.21875
- q_gain: float32 [768], P('head'), may hold values from 0.1 to 1.9
- k_gain: float32 [768], P('head'), may hold values from 0.1 to 1.9
- w_out: bfloat16 [768, 768], P('head'), may hold values from -0.21875 to 0.21875
- seg_len: int32 [16], replicated, may hold values from 512 to 4096, as said below
- dilation: int32 [16], replicated, may hold values from 1 to 16, as said below
- slide_len: int32 [16], P('groups'), parts along dimension 0, may hold values from 1 to 2048, 4096 in all
- reports: bfloat16 [256, 768], P(None, 'head'), may hold values from -6 to 6
- pairs: int32 [16], P('groups'), parts along dimension 0, may hold values from 0 to 255
- log_scale: float32 [1], replicated, may hold values from 2.3 to 3.4
Outputs:
- mixed: bfloat16 [8192, 768], P(('groups', 'ctx', 'sub'), 'head'), parts along dimension 0
- similarity: float32 [16, 256], P('groups'), parts along dimension 0
- loss: float32 [16], P('groups'), parts along dimension 0
There are 2 independent parts, one for each index of `groups`. A program takes and returns all parts, laid end to end along the dimension named above; an argument that names none is the same for every part. Nothing has to cross between parts.
Inputs may be any that keep to these rules, and one draw needn't show every extreme that they name: `seg_len`: each is 512 times a power of two; one head's is 4096. `dilation`: each is a power of two; one head's is 16. `slide_len`: they sum to 4096.
All inputs are finite; a program needn't handle non-finite values.
Results may differ from a plain program's by a relative error of at most 0.0033.
The roundings to bfloat16 on the way count: a program that leaves them out, or rounds other values in their place, can miss the bound.
Values may be sent and summed in bfloat16 or wider, within the bound.
No kernel may reach another device: no remote copies, remote signals or barrier semaphores. Data moves between devices by JAX's collectives and lax.ppermute only.
A program may use at most 64 MiB of HBM per device.

v0:
```python
import math

import jax
import jax.numpy as jnp
from jax import lax
from jax.sharding import PartitionSpec as P

HEAD_DIM = 48
SLIDES = 8
REPORTS = 256


def slide_of(positions, ends):
    return jnp.sum((positions[:, None] >= ends[None, :]).astype(jnp.int32), axis=1)


def head_norm(values, gain):
    scale = lax.rsqrt(jnp.mean(values * values, axis=-1, keepdims=True) + 1e-06)
    return (values * scale * gain).astype(jnp.bfloat16)


def per_device(
    tokens,
    norm_gain,
    w_qkv,
    q_gain,
    k_gain,
    w_out,
    seg_len,
    dilation,
    slide_len,
    reports,
    pairs,
    log_scale,
):
    rows, width = tokens.shape
    local_feat = w_qkv.shape[2]
    heads_dev = local_feat // HEAD_DIM
    head_pos = lax.axis_index("head")
    my_start = lax.axis_index(("ctx", "sub")) * rows
    x_full = tokens.astype(jnp.float32)
    mean_sq = jnp.mean(x_full * x_full, axis=-1, keepdims=True)
    normed = (x_full * lax.rsqrt(mean_sq + 1e-06) * norm_gain).astype(jnp.bfloat16)
    qkv = jnp.dot(normed, w_qkv.reshape(width, 3 * local_feat), preferred_element_type=jnp.float32)
    qkv = qkv.reshape(rows, 3, heads_dev, HEAD_DIM)
    qn = head_norm(qkv[:, 0], q_gain.reshape(heads_dev, HEAD_DIM))
    kflat = head_norm(qkv[:, 1], k_gain.reshape(heads_dev, HEAD_DIM)).reshape(rows, local_feat)
    vflat = qkv[:, 2].astype(jnp.bfloat16).reshape(rows, local_feat)
    glob = head_pos * heads_dev + jnp.arange(heads_dev, dtype=jnp.int32)
    widths = lax.dynamic_slice_in_dim(seg_len, head_pos * heads_dev, heads_dev, 0)
    rates = lax.dynamic_slice_in_dim(dilation, head_pos * heads_dev, heads_dev, 0)
    offsets = jnp.remainder(glob, rates)
    ends = jnp.cumsum(slide_len)
    qpos = my_start + jnp.arange(rows, dtype=jnp.int32)
    qsid = slide_of(qpos, ends)
    qsel = jnp.remainder(qpos[None, :], rates[:, None]) == offsets[:, None]
    qseg = qpos[None, :] // widths[:, None]
    seg_first = my_start // widths * widths
    inv_root = 1.0 / math.sqrt(HEAD_DIM)
    init = (
        jnp.zeros((rows, heads_dev, HEAD_DIM), jnp.float32),
        jnp.zeros((rows, heads_dev), jnp.float32),
    )
    kpiece = lax.all_gather(kflat, ("ctx", "sub"), axis=0, tiled=True)
    vpiece = lax.all_gather(vflat, ("ctx", "sub"), axis=0, tiled=True)
    kstart = jnp.int32(0)
    count = kpiece.shape[0]
    blk = math.gcd(count, 512)
    needed = jnp.any((kstart < seg_first + widths) & (kstart + count > seg_first))

    def run(state):

        def step(j, inner):
            numer, total = inner
            kb = lax.dynamic_slice_in_dim(kpiece, j * blk, blk, 0).reshape(blk, heads_dev, HEAD_DIM)
            vb = lax.dynamic_slice_in_dim(vpiece, j * blk, blk, 0).reshape(blk, heads_dev, HEAD_DIM)
            kpos = j * blk + jnp.arange(blk, dtype=jnp.int32)
            ksid = slide_of(kpos, ends)
            ksel = jnp.remainder(kpos[None, :], rates[:, None]) == offsets[:, None]
            kseg = kpos[None, :] // widths[:, None]
            scores = (
                jnp.einsum("qhd,khd->hqk", qn, kb, preferred_element_type=jnp.float32) * inv_root
            )
            allowed = (
                qsel[:, :, None]
                & ksel[:, None, :]
                & (qseg[:, :, None] == kseg[:, None, :])
                & (qsid[None, :, None] == ksid[None, None, :])
            )
            expo = jnp.where(allowed, jnp.exp(scores), jnp.float32(0.0))
            total = total + jnp.sum(expo, axis=2).T
            numer = numer + jnp.einsum(
                "hqk,khd->qhd", expo.astype(jnp.bfloat16), vb, preferred_element_type=jnp.float32
            )
            return (numer, total)

        return lax.fori_loop(0, count // blk, step, state)

    numer, total = lax.cond(needed, run, lambda state: state, init)
    safe = jnp.where(total > 0, total, jnp.float32(1.0))
    head_out = jnp.where(total[:, :, None] > 0, numer / safe[:, :, None], jnp.float32(0.0))
    head_out = head_out.astype(jnp.bfloat16).reshape(rows, local_feat)
    cols = width // lax.axis_size("head")
    terms = jnp.dot(head_out, w_out, preferred_element_type=jnp.float32)
    proj = lax.psum_scatter(
        terms.astype(jnp.bfloat16), "head", scatter_dimension=1, tiled=True
    ).astype(jnp.float32)
    x_cols = lax.dynamic_slice_in_dim(x_full, head_pos * cols, cols, 1)
    mixed = (x_cols + proj).astype(jnp.bfloat16)
    onehot = (qsid[None, :] == jnp.arange(SLIDES, dtype=jnp.int32)[:, None]).astype(jnp.bfloat16)
    partial_sums = jnp.dot(onehot, mixed, preferred_element_type=jnp.float32)
    sums = lax.psum(partial_sums, ("ctx", "sub"))
    pooled = sums / slide_len.astype(jnp.float32)[:, None]
    rep = reports.astype(jnp.float32)
    dots_part = jnp.dot(pooled, rep.T, precision=lax.Precision.HIGHEST)
    slide_part = jnp.sum(pooled * pooled, axis=1)
    report_part = jnp.sum(rep * rep, axis=1)
    dots, slide_sq, report_sq = lax.psum((dots_part, slide_part, report_part), "head")
    scale = jnp.exp(log_scale[0])
    similarity = scale * dots / jnp.sqrt((slide_sq[:, None] + 1e-06) * (report_sq[None, :] + 1e-06))
    total_exp = jnp.sum(jnp.exp(similarity - scale), axis=1)
    picked = jnp.sum(
        jnp.where(
            jnp.arange(REPORTS, dtype=jnp.int32)[None, :] == pairs[:, None],
            similarity,
            jnp.float32(0.0),
        ),
        axis=1,
    )
    loss = scale + jnp.log(total_exp) - picked
    return (mixed, similarity, loss)


def solution(mesh):
    in_specs = (
        P(("groups", "ctx", "sub"), None),
        P(),
        P(None, None, "head"),
        P("head"),
        P("head"),
        P("head", None),
        P(),
        P(),
        P("groups"),
        P(None, "head"),
        P("groups"),
        P(),
    )
    out_specs = (P(("groups", "ctx", "sub"), "head"), P("groups", None), P("groups"))
    return jax.shard_map(
        per_device, mesh=mesh, in_specs=in_specs, out_specs=out_specs, check_vma=False
    )
```

profile of v0, /device:TPU:0, one launch (start us, length us, event | category | flops | bytes accessed | tf_op | source)
XLA Modules:
  0.0 298.8 jit_solution(12019305275715738126)
XLA Ops:
  7.2 4.0 %copy.21 = bf16[768,3,384]{0,2,1:T(8,128)(2,1)} copy(bf16[768,3,384]{2,0,1:T(8,128)(2,1)} %param.22) | data formatting | bytes 3538944 | tf_op args[2]
  11.5 2.9 fusion.26
  14.6 0.9 fusion.29
  15.6 0.8 slice.23
  16.9 0.8 and_reduce_fusion
  19.1 37.5 %all-gather.5.cloned.1.call-done = bf16[4096,384]{0,1:T(8,128)(2,1)} async-done(((bf16[512,384]{0,1:T(8,128)(2,1)}), bf16[4096,384]{0,1:T(8,128)(2,1)}) %all-gather.5.cloned.1.call-update) | async-done | bytes 3145744 | tf_op jit(solution)/shard_map/all_gather | solution.py:64
  56.6 39.3 %all-gather.3.cloned.1.call-done = bf16[4096,384]{0,1:T(8,128)(2,1)} async-done(((bf16[512,384]{0,1:T(8,128)(2,1)}), bf16[4096,384]{0,1:T(8,128)(2,1)}) %all-gather.3.cloned.1.call-update) | async-done | bytes 3145744 | tf_op jit(solution)/shard_map/all_gather | solution.py:65
  96.1 138.3 %conditional.1 = (f32[512,8,48]{0,2,1:T(8,128)}, f32[512,8]{0,1:T(8,128)}) conditional(s32[]{:T(128)} %convert_element_type.58, () %tuple.46, (s32[]{:T(128)}, s32[8]{0:T(128)S(1)}, s32[8]{0:T(128)S(1)}, s32[8]{0:T(128)S(1)}, s32[8,512]{1,0:T(8,128)S(1)}, /*index=5*/bf16[4096,384]{0,1:T(8,128)(2,1)}, s32[512]{0:T(512)S(1)}, s32[8]{0:T(128)S(1)}, ...), branch_computations={%region_6.9_spmd, %region_7.14_spmd.clone} | conditional | flops 432800928 | bytes 22266784 | solution.py:99
  96.5 137.9 %while.25 = (s32[]{:T(128)}, f32[512,8,48]{0,2,1:T(8,128)}, f32[512,8]{0,1:T(8,128)}, bf16[4096,384]{0,1:T(8,128)(2,1)}, pred[8,512]{1,0:T(8,128)(4,1)S(1)}, /*i...) while((s32[]{:T(128)}, f32[512,8,48]{0,2,1:T(8,128)}, ...), condition=%wide.region_11.13_spmd.clone, body=%wide.region_8.12_spmd.clone.sunk | while | flops 432747584 | bytes 22078000 | solution.py:97
  96.9 1.2 constant_dynamic-slice_fusion.3
  98.6 7.0 %fusion.62 = (f32[8,512]{1,0:T(8,128)S(1)}, f32[8,512,512]{2,1,0:T(8,128)}) fusion(s32[8,512]{1,0:T(8,128)S(1)} %add_select_fusion.4, s32[8,512]{1,0:T(8,128)S(1)} %get-tuple-element.692, pred[512,512]{0,1:T(8,128)(4,1)S(1)} %broadcast_compare_fusion.3, pred[8,512]{1,0:T(8,128)(4,1)S(1)} %fusion.61, pred[8,512]{1,0:T(8,128)(4,1)S(1)} %get-tuple-element.689, ...), kind=kOutput, calls=%fused_computation.1.clone.1 | convolution fusion | flops 216002560 | bytes 9494528 | tf_op jit(solution)/shard_map/cond/branch_1_fun/while/body/eval_jaxpr/qhd,khd->hqk/dot_general | solution.py:82
  105.7 6.9 %fusion.63 = f32[512,8,48]{0,2,1:T(8,128)} fusion(bf16[512,8,48]{0,2,1:T(8,128)(2,1)S(1)} %bitcast.126, f32[8,512,512]{2,1,0:T(8,128)} %get-tuple-element.649, s32[8,512]{1,0:T(8,128)S(1)} %add_select_fusion.4, s32[8,512]{1,0:T(8,128)S(1)} %get-tuple-element.692, pred[512,512]{0,1:T(8,128)(4,1)S(1)} %broadcast_compare_fusion.3, ...), kind=kOutput, calls=%fused_computation.8.clone.1 | convolution fusion | flops 216399872 | bytes 10657793 | tf_op jit(solution)/shard_map/cond/branch_1_fun/while/body/eval_jaxpr/hqk,khd->qhd/dot_general | solution.py:92
  113.4 1.2 constant_dynamic-slice_fusion.3
  115.2 7.0 %fusion.62 = (f32[8,512]{1,0:T(8,128)S(1)}, f32[8,512,512]{2,1,0:T(8,128)}) fusion(s32[8,512]{1,0:T(8,128)S(1)} %add_select_fusion.4, s32[8,512]{1,0:T(8,128)S(1)} %get-tuple-element.692, pred[512,512]{0,1:T(8,128)(4,1)S(1)} %broadcast_compare_fusion.3, pred[8,512]{1,0:T(8,128)(4,1)S(1)} %fusion.61, pred[8,512]{1,0:T(8,128)(4,1)S(1)} %get-tuple-element.689, ...), kind=kOutput, calls=%fused_computation.1.clone.1 | convolution fusion | flops 216002560 | bytes 9494528 | tf_op jit(solution)/shard_map/cond/branch_1_fun/while/body/eval_jaxpr/qhd,khd->hqk/dot_general | solution.py:82
  122.3 6.9 %fusion.63 = f32[512,8,48]{0,2,1:T(8,128)} fusion(bf16[512,8,48]{0,2,1:T(8,128)(2,1)S(1)} %bitcast.126, f32[8,512,512]{2,1,0:T(8,128)} %get-tuple-element.649, s32[8,512]{1,0:T(8,128)S(1)} %add_select_fusion.4, s32[8,512]{1,0:T(8,128)S(1)} %get-tuple-element.692, pred[512,512]{0,1:T(8,128)(4,1)S(1)} %broadcast_compare_fusion.3, ...), kind=kOutput, calls=%fused_computation.8.clone.1 | convolution fusion | flops 216399872 | bytes 10657793 | tf_op jit(solution)/shard_map/cond/branch_1_fun/while/body/eval_jaxpr/hqk,khd->qhd/dot_general | solution.py:92
  129.1 1.3 bitcast_add_fusion.2
  130.8 1.2 constant_dynamic-slice_fusion.3
  132.5 7.0 %fusion.62 = (f32[8,512]{1,0:T(8,128)S(1)}, f32[8,512,512]{2,1,0:T(8,128)}) fusion(s32[8,512]{1,0:T(8,128)S(1)} %add_select_fusion.4, s32[8,512]{1,0:T(8,128)S(1)} %get-tuple-element.692, pred[512,512]{0,1:T(8,128)(4,1)S(1)} %broadcast_compare_fusion.3, pred[8,512]{1,0:T(8,128)(4,1)S(1)} %fusion.61, pred[8,512]{1,0:T(8,128)(4,1)S(1)} %get-tuple-element.689, ...), kind=kOutput, calls=%fused_computation.1.clone.1 | convolution fusion | flops 216002560 | bytes 9494528 | tf_op jit(solution)/shard_map/cond/branch_1_fun/while/body/eval_jaxpr/qhd,khd->hqk/dot_general | solution.py:82
  139.6 6.9 %fusion.63 = f32[512,8,48]{0,2,1:T(8,128)} fusion(bf16[512,8,48]{0,2,1:T(8,128)(2,1)S(1)} %bitcast.126, f32[8,512,512]{2,1,0:T(8,128)} %get-tuple-element.649, s32[8,512]{1,0:T(8,128)S(1)} %add_select_fusion.4, s32[8,512]{1,0:T(8,128)S(1)} %get-tuple-element.692, pred[512,512]{0,1:T(8,128)(4,1)S(1)} %broadcast_compare_fusion.3, ...), kind=kOutput, calls=%fused_computation.8.clone.1 | convolution fusion | flops 216399872 | bytes 10657793 | tf_op jit(solution)/shard_map/cond/branch_1_fun/while/body/eval_jaxpr/hqk,khd->qhd/dot_general | solution.py:92
  146.5 1.3 bitcast_add_fusion.2
  148.1 1.2 constant_dynamic-slice_fusion.3
  149.9 7.0 %fusion.62 = (f32[8,512]{1,0:T(8,128)S(1)}, f32[8,512,512]{2,1,0:T(8,128)}) fusion(s32[8,512]{1,0:T(8,128)S(1)} %add_select_fusion.4, s32[8,512]{1,0:T(8,128)S(1)} %get-tuple-element.692, pred[512,512]{0,1:T(8,128)(4,1)S(1)} %broadcast_compare_fusion.3, pred[8,512]{1,0:T(8,128)(4,1)S(1)} %fusion.61, pred[8,512]{1,0:T(8,128)(4,1)S(1)} %get-tuple-element.689, ...), kind=kOutput, calls=%fused_computation.1.clone.1 | convolution fusion | flops 216002560 | bytes 9494528 | tf_op jit(solution)/shard_map/cond/branch_1_fun/while/body/eval_jaxpr/qhd,khd->hqk/dot_general | solution.py:82
  156.9 6.9 %fusion.63 = f32[512,8,48]{0,2,1:T(8,128)} fusion(bf16[512,8,48]{0,2,1:T(8,128)(2,1)S(1)} %bitcast.126, f32[8,512,512]{2,1,0:T(8,128)} %get-tuple-element.649, s32[8,512]{1,0:T(8,128)S(1)} %add_select_fusion.4, s32[8,512]{1,0:T(8,128)S(1)} %get-tuple-element.692, pred[512,512]{0,1:T(8,128)(4,1)S(1)} %broadcast_compare_fusion.3, ...), kind=kOutput, calls=%fused_computation.8.clone.1 | convolution fusion | flops 216399872 | bytes 10657793 | tf_op jit(solution)/shard_map/cond/branch_1_fun/while/body/eval_jaxpr/hqk,khd->qhd/dot_general | solution.py:92
  163.8 1.3 bitcast_add_fusion.2
  165.4 1.2 constant_dynamic-slice_fusion.3
  167.2 7.0 %fusion.62 = (f32[8,512]{1,0:T(8,128)S(1)}, f32[8,512,512]{2,1,0:T(8,128)}) fusion(s32[8,512]{1,0:T(8,128)S(1)} %add_select_fusion.4, s32[8,512]{1,0:T(8,128)S(1)} %get-tuple-element.692, pred[512,512]{0,1:T(8,128)(4,1)S(1)} %broadcast_compare_fusion.3, pred[8,512]{1,0:T(8,128)(4,1)S(1)} %fusion.61, pred[8,512]{1,0:T(8,128)(4,1)S(1)} %get-tuple-element.689, ...), kind=kOutput, calls=%fused_computation.1.clone.1 | convolution fusion | flops 216002560 | bytes 9494528 | tf_op jit(solution)/shard_map/cond/branch_1_fun/while/body/eval_jaxpr/qhd,khd->hqk/dot_general | solution.py:82
  174.2 6.9 %fusion.63 = f32[512,8,48]{0,2,1:T(8,128)} fusion(bf16[512,8,48]{0,2,1:T(8,128)(2,1)S(1)} %bitcast.126, f32[8,512,512]{2,1,0:T(8,128)} %get-tuple-element.649, s32[8,512]{1,0:T(8,128)S(1)} %add_select_fusion.4, s32[8,512]{1,0:T(8,128)S(1)} %get-tuple-element.692, pred[512,512]{0,1:T(8,128)(4,1)S(1)} %broadcast_compare_fusion.3, ...), kind=kOutput, calls=%fused_computation.8.clone.1 | convolution fusion | flops 216399872 | bytes 10657793 | tf_op jit(solution)/shard_map/cond/branch_1_fun/while/body/eval_jaxpr/hqk,khd->qhd/dot_general | solution.py:92
  181.1 1.3 bitcast_add_fusion.2
  182.7 1.2 constant_dynamic-slice_fusion.3
  184.5 7.0 %fusion.62 = (f32[8,512]{1,0:T(8,128)S(1)}, f32[8,512,512]{2,1,0:T(8,128)}) fusion(s32[8,512]{1,0:T(8,128)S(1)} %add_select_fusion.4, s32[8,512]{1,0:T(8,128)S(1)} %get-tuple-element.692, pred[512,512]{0,1:T(8,128)(4,1)S(1)} %broadcast_compare_fusion.3, pred[8,512]{1,0:T(8,128)(4,1)S(1)} %fusion.61, pred[8,512]{1,0:T(8,128)(4,1)S(1)} %get-tuple-element.689, ...), kind=kOutput, calls=%fused_computation.1.clone.1 | convolution fusion | flops 216002560 | bytes 9494528 | tf_op jit(solution)/shard_map/cond/branch_1_fun/while/body/eval_jaxpr/qhd,khd->hqk/dot_general | solution.py:82
  191.6 6.9 %fusion.63 = f32[512,8,48]{0,2,1:T(8,128)} fusion(bf16[512,8,48]{0,2,1:T(8,128)(2,1)S(1)} %bitcast.126, f32[8,512,512]{2,1,0:T(8,128)} %get-tuple-element.649, s32[8,512]{1,0:T(8,128)S(1)} %add_select_fusion.4, s32[8,512]{1,0:T(8,128)S(1)} %get-tuple-element.692, pred[512,512]{0,1:T(8,128)(4,1)S(1)} %broadcast_compare_fusion.3, ...), kind=kOutput, calls=%fused_computation.8.clone.1 | convolution fusion | flops 216399872 | bytes 10657793 | tf_op jit(solution)/shard_map/cond/branch_1_fun/while/body/eval_jaxpr/hqk,khd->qhd/dot_general | solution.py:92
  198.4 1.3 bitcast_add_fusion.2
  200.0 1.2 constant_dynamic-slice_fusion.3
  201.8 7.0 %fusion.62 = (f32[8,512]{1,0:T(8,128)S(1)}, f32[8,512,512]{2,1,0:T(8,128)}) fusion(s32[8,512]{1,0:T(8,128)S(1)} %add_select_fusion.4, s32[8,512]{1,0:T(8,128)S(1)} %get-tuple-element.692, pred[512,512]{0,1:T(8,128)(4,1)S(1)} %broadcast_compare_fusion.3, pred[8,512]{1,0:T(8,128)(4,1)S(1)} %fusion.61, pred[8,512]{1,0:T(8,128)(4,1)S(1)} %get-tuple-element.689, ...), kind=kOutput, calls=%fused_computation.1.clone.1 | convolution fusion | flops 216002560 | bytes 9494528 | tf_op jit(solution)/shard_map/cond/branch_1_fun/while/body/eval_jaxpr/qhd,khd->hqk/dot_general | solution.py:82
  208.9 6.9 %fusion.63 = f32[512,8,48]{0,2,1:T(8,128)} fusion(bf16[512,8,48]{0,2,1:T(8,128)(2,1)S(1)} %bitcast.126, f32[8,512,512]{2,1,0:T(8,128)} %get-tuple-element.649, s32[8,512]{1,0:T(8,128)S(1)} %add_select_fusion.4, s32[8,512]{1,0:T(8,128)S(1)} %get-tuple-element.692, pred[512,512]{0,1:T(8,128)(4,1)S(1)} %broadcast_compare_fusion.3, ...), kind=kOutput, calls=%fused_computation.8.clone.1 | convolution fusion | flops 216399872 | bytes 10657793 | tf_op jit(solution)/shard_map/cond/branch_1_fun/while/body/eval_jaxpr/hqk,khd->qhd/dot_general | solution.py:92
  215.8 1.3 bitcast_add_fusion.2
  217.4 1.2 constant_dynamic-slice_fusion.3
  219.2 7.0 %fusion.62 = (f32[8,512]{1,0:T(8,128)S(1)}, f32[8,512,512]{2,1,0:T(8,128)}) fusion(s32[8,512]{1,0:T(8,128)S(1)} %add_select_fusion.4, s32[8,512]{1,0:T(8,128)S(1)} %get-tuple-element.692, pred[512,512]{0,1:T(8,128)(4,1)S(1)} %broadcast_compare_fusion.3, pred[8,512]{1,0:T(8,128)(4,1)S(1)} %fusion.61, pred[8,512]{1,0:T(8,128)(4,1)S(1)} %get-tuple-element.689, ...), kind=kOutput, calls=%fused_computation.1.clone.1 | convolution fusion | flops 216002560 | bytes 9494528 | tf_op jit(solution)/shard_map/cond/branch_1_fun/while/body/eval_jaxpr/qhd,khd->hqk/dot_general | solution.py:82
  226.2 6.9 %fusion.63 = f32[512,8,48]{0,2,1:T(8,128)} fusion(bf16[512,8,48]{0,2,1:T(8,128)(2,1)S(1)} %bitcast.126, f32[8,512,512]{2,1,0:T(8,128)} %get-tuple-element.649, s32[8,512]{1,0:T(8,128)S(1)} %add_select_fusion.4, s32[8,512]{1,0:T(8,128)S(1)} %get-tuple-element.692, pred[512,512]{0,1:T(8,128)(4,1)S(1)} %broadcast_compare_fusion.3, ...), kind=kOutput, calls=%fused_computation.8.clone.1 | convolution fusion | flops 216399872 | bytes 10657793 | tf_op jit(solution)/shard_map/cond/branch_1_fun/while/body/eval_jaxpr/hqk,khd->qhd/dot_general | solution.py:92
  233.1 1.3 bitcast_add_fusion.2
  235.1 0.7 broadcast_compare_fusion.1
  235.8 1.2 select_convert_fusion
  237.7 1.2 copy.24
  239.9 15.6 %reduce-scatter.4.cloned.1.call-done = bf16[384,512]{1,0:T(8,128)(2,1)} async-done(((bf16[768,512]{1,0:T(8,128)(2,1)}), bf16[384,512]{1,0:T(8,128)(2,1)}) %reduce-scatter.4.cloned.1.call-update) | async-done | bytes 393232
  255.5 1.2 copy.25
  257.0 28.4 %psum.28 = f32[8,384]{1,0:T(8,128)S(1)} all-reduce(f32[8,384]{1,0:T(8,128)S(1)} %fusion.33), channel_id=1, replica_groups=mesh['groups'=2,'ctx'=4,'head'=2,'sub'=2] {'ctx','sub'}, use_global_device_ids=true, to_apply=%region_13.16 | all-reduce | flops 3072 | bytes 24576 | tf_op jit(solution)/shard_map/psum | solution.py:112
  285.8 5.1 %all-reduce = (f32[8,256]{1,0:T(8,128)S(1)}, f32[256]{0:T(256)S(1)}, f32[8]{0:T(128)S(1)}) all-reduce(f32[8,256]{1,0:T(8,128)S(1)} %fusion.35, f32[256]{0:T(256)S(1)} %multiply_reduce_fusion.3, f32[8]{0:T(128)S(1)} %multiply_reduce_fusion.4), channel_id=1, replica_groups=mesh['groups'=2,'ctx'=4,'head'=2,'sub'=2] {'head'}, use_global_device_ids=true, to_apply=%region_14.17 | all-reduce | flops 2312 | bytes 18496 | tf_op jit(solution)/shard_map/psum | solution.py:118
  290.9 0.8 exponential_reduce_fusion
  (132 shorter events, 12.7 us)
Async XLA Ops:
  7.2 229.9 %copy-start = (bf16[384,768]{1,0:T(8,128)(2,1)S(1)}, bf16[384,768]{1,0:T(8,128)(2,1)}, u32[]{:S(2)}) copy-start(bf16[384,768]{1,0:T(8,128)(2,1)} %param.25) | copy-start | bytes 1769476
  7.2 4.0 %copy-start.1 = (bf16[512,768]{1,0:T(8,128)(2,1)S(1)}, bf16[512,768]{1,0:T(8,128)(2,1)}, u32[]{:S(2)}) copy-start(bf16[512,768]{1,0:T(8,128)(2,1)} %param.20) | copy-start | bytes 2359300
  7.2 4.3 %copy-start.10 = (f32[768]{0:T(1024)S(1)}, f32[768]{0:T(1024)}, u32[]{:S(2)}) copy-start(f32[768]{0:T(1024)} %param.21) | copy-start | bytes 9220
  7.2 49.4 %all-gather.5.cloned.1.call-start = ((), (), s32[]{:S(2)}) async-start(), calls=%async_computation.2 | async-start | bytes 3538944 | tf_op jit(solution)/shard_map/all_gather | solution.py:64
  11.5 3.2 %copy-start.5 = (f32[384]{0:T(512)S(1)}, f32[384]{0:T(512)}, u32[]{:S(2)}) copy-start(f32[384]{0:T(512)} %param.24) | copy-start | bytes 4612
  14.4 2.1 copy-start.11
  14.4 2.2 copy-start.6
  14.4 2.3 copy-start.8
  14.4 2.4 copy-start.9
  15.5 80.4 %all-gather.3.cloned.1.call-start = ((), (), s32[]{:S(2)}) async-start(), calls=%async_computation.1 | async-start | bytes 3538944 | tf_op jit(solution)/shard_map/all_gather | solution.py:65
  16.4 239.1 %reduce-scatter.4.cloned.1.call-start = ((), (), s32[]{:S(2)}) async-start(), calls=%async_computation.3 | async-start | bytes 1179648
  237.1 1.8 copy-start.2
  237.7 2.0 copy-start.4
  238.9 52.0 %copy-start.7 = (s32[8]{0:T(128)S(1)}, s32[8]{0:T(128)}, u32[]{:S(2)}) copy-start(s32[8]{0:T(128)} %param.30) | copy-start | bytes 100
  256.8 35.5 %copy-start.3 = (bf16[512,384]{1,0:T(8,128)(2,1)}, bf16[512,384]{1,0:T(8,128)(2,1)S(1)}, u32[]{:S(2)}) copy-start(bf16[512,384]{1,0:T(8,128)(2,1)S(1)} %add_convert_fusion) | copy-start | bytes 1179652
Sparse Core Ops, SparseCore 0:
  15.6 40.9 all-gather.4
  58.8 37.1 all-gather.2
  239.0 16.4 reduce-scatter.3
where the time goes:
time: 300 us; the launch traced here: 299 us
  matrix products  115 us (38%)
  waiting for transfers between devices  92.5 us (31%)
  blocking collectives  33.4 us (11%)
  other arithmetic  24.9 us (8%)
  local copies, waits for them, and re-layouts  16.8 us (6%)
  between operations  15.4 us (5%)
    dot_general x8, matrix products, step(): jnp.einsum('qhd,khd->hqk', qn, kb, preferred_element_type=jnp.float32)  56.3 us
    dot_general x8, matrix products, step(): jnp.einsum('hqk,khd->qhd', expo.astype(jnp.bfloat16), vb, preferred_eleme...  54.9 us
    all_gather x1, waiting for transfers between devices, per_device(): vpiece = lax.all_gather(vflat, ('ctx', 'sub'), axis=0, tiled=True)  39.3 us
    all_gather x1, waiting for transfers between devices, per_device(): kpiece = lax.all_gather(kflat, ('ctx', 'sub'), axis=0, tiled=True)  37.5 us
    psum x1, blocking collectives, per_device(): sums = lax.psum(partial_sums, ('ctx', 'sub'))  28.4 us
    unnamed x4, waiting for transfers between devices  15.7 us
    add x8, other arithmetic, step(): total = total + jnp.sum(expo, axis=2).T  9.9 us
    dynamic_slice x8, local copies, waits for them, and re-layouts, step(): lax.dynamic_slice_in_dim(kpiece, j * blk, blk, 0)  9.4 us
  transfers between devices with their start and end apart: 3, of which 3 were waited for; matrix products, arithmetic and copies ran while one was open for 1% of the time, Pallas kernels for 0%

commit v1 on v0

v1 whole, which is shorter than its diff:
```python
import functools
import math

import jax
import jax.numpy as jnp
from jax import lax
from jax.experimental import pallas as pl
from jax.experimental.pallas import tpu as pltpu
from jax.sharding import PartitionSpec as P


HEAD_DIM = 48
RES = 16
LANES = 128
HALF = 64
FAR = 4096.0
MIB = 1024 * 1024
F32 = jnp.float32
BF16 = jnp.bfloat16
I32 = jnp.int32


def rev(r):
    return int(f"{r:04b}"[::-1], 2)


def rev_traced(c):
    return ((c & 1) << 3) | ((c & 2) << 1) | ((c >> 1) & 2) | ((c >> 3) & 1)


def dot(a, b, dims=((1,), (0,)), precision=None):
    return lax.dot_general(a, b, (dims, ((), ())), precision=precision, preferred_element_type=F32)


def units_of(dil_ref, h):
    rate = dil_ref[h]
    count = jnp.int32(RES)
    for step in range(1, RES.bit_length()):
        count = jnp.where(rate == 1 << step, RES >> step, count)
    return count


def first_unit(dil_ref, h):
    return rev_traced(jnp.bitwise_and(h, dil_ref[h] - 1))


UNITS, FIRST, OFFSET, REACH, FIELDS = 0, 1, 2, 3, 4
HEAD_AT = 4


def slide_tiles(len_ref, rows, my_start, slides, one, inside, outside):
    per = rows // RES
    base = RES * lax.broadcasted_iota(I32, (per, LANES), 0) + my_start
    lane = lax.broadcasted_iota(I32, (1, LANES), 1)
    tiles = []
    for side in range(2):
        low, high, on = slide_lanes(len_ref, S_AT[side], slides)
        high = jnp.where(on, high, -1)
        other = jnp.where(on, outside, jnp.where(lane == ONE_AT, one, 0.0))
        parts = []
        for u in range(RES):
            tok = base + rev(u)
            parts.append(jnp.where((tok >= low) & (tok < high), inside, other))
        tiles.append(jnp.concatenate(parts, axis=0))
    return tiles


def slide_lanes(ends_ref, base, slides):
    lane = lax.broadcasted_iota(I32, (1, LANES), 1) - base
    low = jnp.zeros((1, LANES), I32)
    high = jnp.zeros((1, LANES), I32)
    end = jnp.int32(0)
    for s in range(slides):
        low = jnp.where(lane == s, end, low)
        end = end + ends_ref[s]
        high = jnp.where(lane == s, end, high)
    return low, high, (lane >= 0) & (lane < slides)


def selector(source, first, heads_at, target):
    lane = lax.broadcasted_iota(I32, (1, 2 * LANES), 1)
    wanted = jnp.full((1, 2 * LANES), -1, I32)
    for side in range(2):
        at = side * LANES + target[side]
        inside = (lane >= at) & (lane < at + HEAD_DIM)
        wanted = jnp.where(inside, (heads_at + side) * HEAD_DIM - first + lane - at, wanted)
    row = lax.broadcasted_iota(I32, (source, 2 * LANES), 0)
    return jnp.where(row == wanted, 1.0, 0.0).astype(BF16)


V_AT = (0, HALF)
K_AT = (HALF, 0)
S_AT = (HALF + HEAD_DIM, HEAD_DIM)
ONE_AT = HALF - 1


def head_scale(values, feat):
    sq = values * values
    high = sq.astype(BF16)
    low = (sq - high.astype(F32)).astype(BF16)
    lane = lax.broadcasted_iota(I32, (1, feat), 1)
    first = jnp.zeros((1, feat), I32)
    for h in range(1, feat // HEAD_DIM):
        first = jnp.where(lane >= h * HEAD_DIM, h * HEAD_DIM, first)
    row = lax.broadcasted_iota(I32, (feat, feat), 0)
    same = jnp.where((row >= first) & (row < first + HEAD_DIM), 1.0, 0.0).astype(BF16)
    return lax.rsqrt((dot(high, same) + dot(low, same)) * (1.0 / HEAD_DIM) + 1e-06)


def span(pair, feat):
    first = pair * 2 * HEAD_DIM // LANES * LANES
    last = ((pair + 1) * 2 * HEAD_DIM - 1) // LANES * LANES + LANES
    return first, min(last, feat) - first


def members(slide_ref, tok, slides):
    row = lax.broadcasted_iota(I32, (slides, 1), 0)
    low = jnp.zeros((slides, 1), I32)
    high = jnp.zeros((slides, 1), I32)
    end = jnp.int32(0)
    for s in range(slides):
        low = jnp.where(row == s, end, low)
        end = end + slide_ref[s]
        high = jnp.where(row == s, end, high)
    return jnp.where((tok >= low) & (tok < high), 1.0, 0.0).astype(BF16)


def keys_kernel(
    ladder, heads, parts, classes, slides, seg_ref, dil_ref, len_ref, x_ref, ng_ref, wk_ref, wv_ref, kg_ref,
    pack_ref, normed_ref, meta_ref, xs_ref, kv_ref,
):
    rows, width = x_ref.shape
    feat = heads * HEAD_DIM
    per = rows // RES
    base = lax.axis_index("head") * heads
    my_start = lax.axis_index(("ctx", "sub")) * rows
    segs = [seg_ref[h] for h in range(parts * heads)]
    counts = [units_of(dil_ref, h) for h in range(parts * heads)]
    fits = [jnp.bool_(True) for _ in ladder]
    for c in range(1, classes + 1):
        most = jnp.int32(0)
        for part in range(parts):
            total = jnp.int32(0)
            for h in range(part * heads, (part + 1) * heads):
                total = total + jnp.where(segs[h] >= (rows << c), counts[h], 0)
            most = jnp.maximum(most, total)
        for i, caps in enumerate(ladder):
            fits[i] = fits[i] & (most <= caps[min(c, len(caps)) - 1])
    tier = jnp.int32(len(ladder) - 1)
    for i in reversed(range(len(ladder))):
        tier = jnp.where(fits[i], i, tier)
    meta_ref[0] = tier
    local_seg = [seg_ref[base + h] for h in range(heads)]
    local_units = [units_of(dil_ref, base + h) for h in range(heads)]
    starts = [first_unit(dil_ref, base + h) for h in range(heads)]
    offset = []
    for h in range(heads):
        total = jnp.int32(0)
        for other in range(heads):
            ahead = local_seg[other] > local_seg[h]
            if other < h:
                ahead = ahead | (local_seg[other] == local_seg[h])
            if other != h:
                total = total + jnp.where(ahead, local_units[other], 0)
        offset.append(total)
        at = HEAD_AT + h * FIELDS
        meta_ref[at + UNITS] = local_units[h]
        meta_ref[at + FIRST] = starts[h] * per
        meta_ref[at + OFFSET] = total * per
        meta_ref[at + REACH] = local_seg[h] // rows

    x = x_ref[...].astype(F32)
    mean_sq = jnp.mean(x * x, axis=-1, keepdims=True)
    normal = x * lax.rsqrt(mean_sq + 1e-06) * ng_ref[...].reshape(1, width)
    for c in range(width // LANES):
        lanes = slice(c * LANES, (c + 1) * LANES)
        xs_ref[c] = normal[:, lanes]
        for r in range(RES):
            at = rev(r) * per
            normed_ref[at : at + per, lanes] = xs_ref[c, pl.ds(r, per, stride=RES), :].astype(BF16)
    normed = normed_ref[...]
    keys = dot(normed, wk_ref[0])
    vals = dot(normed, wv_ref[0]).astype(BF16)
    kn = (keys * head_scale(keys, feat) * kg_ref[...].reshape(1, feat)).astype(BF16)
    extra = slide_tiles(len_ref, rows, my_start, slides, 1.0, 0.0, -FAR)
    for pair in range(heads // 2):
        first, size = span(pair, feat)
        both = dot(kn[:, first : first + size], selector(size, first, 2 * pair, K_AT))
        both = both + dot(vals[:, first : first + size], selector(size, first, 2 * pair, V_AT))
        for side in range(2):
            h = 2 * pair + side
            kv_ref[h] = (both[:, side * LANES : (side + 1) * LANES] + extra[side]).astype(BF16)

    for h in range(heads):

        def put(u, carry, h=h, to=offset[h], at=starts[h]):
            piece = kv_ref[h, pl.ds(pl.multiple_of((at + u) * per, per), per), :]
            pack_ref[pl.ds(pl.multiple_of((to + u) * per, per), per), :] = piece
            return carry

        lax.fori_loop(0, local_units[h], put, 0)


def queries_kernel(
    heads, slides, blocks, len_ref, x_ref, normed_ref, w_ref, qg_ref, w_out_ref, rep_ref, q_ref, sums_ref, wide_ref
):
    rows = normed_ref.shape[0]
    feat = heads * HEAD_DIM
    my_start = lax.axis_index(("ctx", "sub")) * rows
    piece = rows // 4
    per = rows // RES
    base = RES * lax.broadcasted_iota(I32, (per, LANES), 0) + my_start

    def step(i, carry):
        here = pl.ds(pl.multiple_of(i * piece, piece), piece)
        q = dot(normed_ref[here, :], w_ref[0])
        qn = (q * head_scale(q, feat) * qg_ref[...].reshape(1, feat)).astype(BF16)
        extra = []
        for side in range(2):
            low, high, on = slide_lanes(len_ref, S_AT[side], slides)
            high = jnp.where(on, high, -1)
            parts = []
            for u in range(piece // per):
                tok = base + rev_traced(i * (piece // per) + u)
                parts.append(jnp.where((tok >= low) & (tok < high), 1.0, 0.0))
            extra.append(jnp.concatenate(parts, axis=0))
        for pair in range(heads // 2):
            first, size = span(pair, feat)
            both = dot(qn[:, first : first + size], selector(size, first, 2 * pair, K_AT))
            for side in range(2):
                lanes = slice(side * LANES, (side + 1) * LANES)
                q_ref[2 * pair + side, here, :] = (both[:, lanes] + extra[side]).astype(BF16)
        return carry

    lax.fori_loop(0, rows // piece, step, 0)
    place = lax.broadcasted_iota(I32, (1, rows), 1) + my_start
    width = x_ref.shape[1]
    sums_ref[:, :width] = dot(members(len_ref, place, slides), x_ref[...])
    rep = rep_ref[...].astype(F32)
    share = jnp.full((slides, rep.shape[1]), 1.0 / blocks, F32)
    sums_ref[:, width:] = dot(share, rep * rep, ((1,), (1,)), lax.Precision.HIGHEST)
    wide_ref[...] = jnp.zeros_like(wide_ref)
    for h in range(heads):
        at = h // 2 * LANES + V_AT[h % 2]
        wide_ref[at : at + HEAD_DIM, :] = w_out_ref[h * HEAD_DIM : (h + 1) * HEAD_DIM, :]


def attend_kernel(heads, blocks, slides, meta_ref, len_ref, q_ref, *rest):
    kv_refs = rest[:blocks]
    out_ref, kvs_ref, keys_ref, acc_ref, list_ref, before_ref, sem = rest[blocks:]
    rows = q_ref.shape[1]
    per = rows // RES
    me = lax.axis_index(("ctx", "sub"))
    copies = []
    for m in range(blocks):
        size = kv_refs[m].shape[0]
        copies.append(pltpu.make_async_copy(kv_refs[m], kvs_ref.at[m, pl.ds(0, size), :], sem.at[m]))
        copies[-1].start()
    low = jnp.int32(0)
    high = jnp.int32(rows * blocks)
    end = jnp.int32(0)
    for s in range(slides):
        end = end + len_ref[s]
        low = jnp.where(end <= me * rows, jnp.maximum(low, end), low)
        high = jnp.where(end >= (me + 1) * rows, jnp.minimum(high, end), high)
    count = jnp.int32(0)
    for m in range(blocks):
        other = jnp.bitwise_xor(me, m) * rows
        before_ref[m] = count
        list_ref[count] = jnp.int32(m)
        count = count + ((other < high) & (other + rows > low)).astype(I32)
    before_ref[blocks] = count
    out_ref[...] = jnp.zeros_like(out_ref)
    lane = lax.broadcasted_iota(I32, (1, LANES), 1)
    outside = jnp.zeros((1, LANES), jnp.bool_)
    for side in range(2):
        outside = outside | ((lane >= S_AT[side]) & (lane < S_AT[side] + slides))
    nothing = jnp.where(outside, -FAR, 0.0)
    for copy in copies:
        copy.wait()
    factor = math.log2(math.e) / math.sqrt(HEAD_DIM)

    def head_step(h, carry):
        entry = HEAD_AT + h * FIELDS
        units = meta_ref[entry + UNITS]
        first = meta_ref[entry + FIRST]
        off = meta_ref[entry + OFFSET]
        some = before_ref[meta_ref[entry + REACH]]
        pair = h >> 1
        side = h & 1

        def attend(u, steps):
            size = u * per
            tile = min(size * 8, rows)
            group = tile // size
            parts = some * steps
            tiles = (parts + (group - 1)) >> (group.bit_length() - 1)
            ours = (lane >= HALF) == (side == 1)

            def take(i, carry):
                block = lax.shift_right_logical(i, steps - 1)
                at = off + (i & (steps - 1)) * size
                keys_ref[pl.ds(pl.multiple_of(i * size, size), size), :] = kvs_ref[
                    list_ref[block], pl.ds(pl.multiple_of(at, per), size), :
                ]
                return carry

            def fill(i, carry):
                keys_ref[pl.ds(pl.multiple_of(i * size, size), size), :] = jnp.broadcast_to(
                    nothing, (size, LANES)
                ).astype(BF16)
                return carry

            lax.fori_loop(0, parts, take, 0)
            lax.fori_loop(parts, tiles * group, fill, 0)

            def q_step(i, carry):
                here = pl.ds(pl.multiple_of(first + i * size, per), size)
                q = q_ref[h, here, :]
                acc_ref[0:size, :] = jnp.zeros((size, LANES), F32)

                def k_step(t, carry):
                    kv = keys_ref[pl.ds(pl.multiple_of(t * tile, tile), tile), :]
                    e = jnp.exp2(dot(q, kv, ((1,), (1,))) * factor)
                    acc_ref[0:size, :] += dot(e.astype(BF16), kv)
                    return carry

                lax.fori_loop(0, tiles, k_step, 0)
                acc = acc_ref[0:size, :]
                total = acc[:, ONE_AT : ONE_AT + 1]
                safe = jnp.where(total > 0, total, 1.0)
                res = jnp.where(total > 0, acc / safe, 0.0).astype(BF16)
                out_ref[pair, here, :] = jnp.where(ours, res, out_ref[pair, here, :])
                return carry

            lax.fori_loop(0, steps, q_step, 0)

        for u in (1, 2, 4):
            pl.when(units == u)(functools.partial(attend, u, jnp.int32(1)))
        pl.when(units >= 8)(functools.partial(attend, 8, units >> 3))
        return carry

    lax.fori_loop(0, heads, head_step, 0)


def away_kernel(slides, len_ref, tok_sums_ref, out_ref, wide_ref, terms_ref, sums_ref):
    pairs, rows, _ = out_ref.shape
    width = wide_ref.shape[1]
    cols = terms_ref.shape[1]
    half = lax.axis_index("head")
    my_start = lax.axis_index(("ctx", "sub")) * rows
    tok = lax.broadcasted_iota(I32, (1, rows), 1)
    per = rows // RES
    tok = my_start + RES * (tok & (per - 1)) + rev_traced(tok // per)
    member = members(len_ref, tok, slides)
    if cols == width:
        columns = slice(None)
        own = jnp.broadcast_to(half == 0, (1, width))
    else:
        columns = pl.ds(pl.multiple_of((1 - half) * cols, LANES), cols)
        lane = lax.broadcasted_iota(I32, (1, width), 1)
        own = (lane >= half * cols) & (lane < half * cols + cols)
    sums = jnp.where(own, tok_sums_ref[:, :width], 0.0)
    for pair in range(pairs):
        pooled = dot(member, out_ref[pair])
        top = pooled.astype(BF16)
        rest = (pooled - top.astype(F32)).astype(BF16)
        both = dot(jnp.concatenate([top, rest], axis=0), wide_ref[pair * LANES : (pair + 1) * LANES, :])
        sums = sums + both[:slides] + both[slides:]
    sums_ref[:, :width] = sums
    sums_ref[:, width:] = tok_sums_ref[:, width:]
    out = jnp.concatenate([out_ref[pair] for pair in range(pairs)], axis=1)
    terms_ref[...] = dot(out, wide_ref[:, columns]).astype(BF16)


def mix_kernel(x_ref, out_ref, wide_ref, got_ref, mixed_ref, p_ref):
    pairs, rows, _ = out_ref.shape
    per = rows // RES
    cols = got_ref.shape[1]
    mine = pl.multiple_of(lax.axis_index("head") * cols, LANES)
    out = jnp.concatenate([out_ref[pair] for pair in range(pairs)], axis=1)
    acc = got_ref[...].astype(F32) + dot(out, wide_ref[:, pl.ds(mine, cols)])
    for c in range(cols // LANES):
        lanes = slice(c * LANES, (c + 1) * LANES)
        for r in range(RES):
            at = rev(r) * per
            p_ref[c, pl.ds(r, per, stride=RES), :] = acc[at : at + per, lanes]
        x = x_ref[:, pl.ds(pl.multiple_of(mine + c * LANES, LANES), LANES)]
        mixed_ref[:, lanes] = (x.astype(F32) + p_ref[c]).astype(BF16)


def loss_kernel(swapped, len_ref, pairs_ref, scale_ref, sums_ref, other_ref, *rest):
    reps, (sim_ref, loss_ref) = rest[:-2], rest[-2:]
    slides = sums_ref.shape[0]
    bank, cols = reps[0].shape
    width = sums_ref.shape[1] - bank
    row = lax.broadcasted_iota(I32, (slides, 1), 0)
    count = jnp.zeros((slides, 1), I32)
    pick = jnp.zeros((slides, 1), I32)
    for s in range(slides):
        count = jnp.where(row == s, len_ref[s], count)
        pick = jnp.where(row == s, pairs_ref[s], pick)
    dots = jnp.zeros((slides, bank), F32)
    ss = jnp.zeros((slides, 1), F32)
    for i, rep in enumerate(reps):
        at = pl.ds(0, cols)
        if swapped:
            half = lax.axis_index("head")
            at = pl.ds(pl.multiple_of((half if i == 0 else 1 - half) * cols, LANES), cols)
        sums = sums_ref[:, at]
        if swapped:
            sums = sums + other_ref[:, at]
        pooled = sums / count.astype(F32)
        ss = ss + jnp.sum(pooled * pooled, axis=1, keepdims=True)
        pieces = []
        left = pooled
        for _ in range(3):
            pieces.append(left.astype(BF16))
            left = left - pieces[-1].astype(F32)
        both = dot(jnp.concatenate(pieces, axis=0), rep[...], ((1,), (1,)))
        dots = dots + both[:slides] + both[slides : 2 * slides] + both[2 * slides :]
    rr = sums_ref[:, width:]
    if swapped:
        rr = rr + other_ref[:, width:]
    scale = jnp.exp(jnp.full((1, 1), scale_ref[0], F32))
    sim = scale * dots / jnp.sqrt((ss + 1e-06) * (rr + 1e-06))
    sim_ref[...] = sim
    total = jnp.sum(jnp.exp(sim - scale), axis=1, keepdims=True)
    lane = lax.broadcasted_iota(I32, (slides, bank), 1)
    picked = jnp.sum(jnp.where(lane == pick, sim, 0.0), axis=1, keepdims=True)
    loss = scale + jnp.log(total) - picked
    here = lax.broadcasted_iota(I32, (slides, slides), 0) == lax.broadcasted_iota(I32, (slides, slides), 1)
    loss_ref[...] = jnp.sum(jnp.where(here, loss, 0.0), axis=0)


SMEM = pl.BlockSpec(memory_space=pltpu.SMEM)
VMEM = pl.BlockSpec(memory_space=pltpu.VMEM)
ANY = pl.BlockSpec(memory_space=pl.ANY)


def call(kernel, out_shape, in_specs, out_specs, scratch=(), grid=(), vmem=16, flops=1000000, moved=1000000):
    return pl.pallas_call(
        kernel,
        grid=grid,
        out_shape=out_shape,
        in_specs=in_specs,
        out_specs=out_specs,
        scratch_shapes=list(scratch),
        compiler_params=pltpu.CompilerParams(vmem_limit_bytes=vmem * MIB),
        cost_estimate=pl.CostEstimate(flops=flops, bytes_accessed=moved, transcendentals=0),
    )


def ladder_of(full):
    steps = ((64, 24, 8), (64, 32, 12), (64, 24, 16), (64, 40, 16), (64, 32, 24), (96, 48, 24), (96, 48, 32), (96, 64, 40))
    fitting = tuple(step for step in steps if step[0] < full)
    return fitting + ((full, full, full),)


def plane(w3, which):
    return pl.BlockSpec((1,) + w3.shape[1:], lambda i: (which, 0, 0))


def run_device(
    tokens, norm_gain, w_qkv, q_gain, k_gain, w_out, seg_len, dilation, slide_len, reports, pairs, log_scale
):
    rows, width = tokens.shape
    feat = w_qkv.shape[2]
    heads = feat // HEAD_DIM
    slides = slide_len.shape[0]
    per = rows // RES
    nz, ns, nx = lax.axis_size("ctx"), lax.axis_size("sub"), lax.axis_size("head")
    blocks = nz * ns
    classes = blocks.bit_length() - 1
    full = heads * RES
    ladder = ladder_of(full)
    cols = width // nx
    swap = [(0, 1), (1, 0)]

    w3 = jnp.transpose(w_qkv, (1, 0, 2))
    pack, normed, meta = call(
        functools.partial(keys_kernel, ladder, heads, nx, classes, slides),
        (
            jax.ShapeDtypeStruct((full * per, LANES), BF16),
            jax.ShapeDtypeStruct((rows, width), BF16),
            jax.ShapeDtypeStruct((HEAD_AT + heads * FIELDS,), I32),
        ),
        [SMEM, SMEM, SMEM, VMEM, VMEM, plane(w3, 1), plane(w3, 2), VMEM],
        (VMEM, VMEM, SMEM),
        [pltpu.VMEM((width // LANES, rows, LANES), F32), pltpu.VMEM((heads, rows, LANES), BF16)],
        grid=(1,),
    )(seg_len, dilation, slide_len, tokens, norm_gain, w3, w3, k_gain)

    bank = reports.shape[0]

    def branch(caps):
        near, mid, far = (min(c, full) * per for c in caps)

        def run(operands):
            pack, normed, tokens, w3, q_gain, w_out, reports, meta, slide_len = operands
            got = {0: pack}
            for m in range(1, nz):
                ends = [(i, i ^ m) for i in range(nz) if abs(i - (i ^ m)) <= nz // 2]
                got[2 * m] = lax.ppermute(pack[: mid if m == 1 else far], "ctx", ends)
            got[1] = lax.ppermute(pack[:near], "sub", swap)
            if nx == 2:
                rep_got = lax.ppermute(reports, "head", swap)
            else:
                rep_got = lax.all_gather(reports, "head", axis=1, tiled=True)
            q, tok_sums, wide = call(
                functools.partial(queries_kernel, heads, slides, blocks),
                (
                    jax.ShapeDtypeStruct((heads, rows, LANES), BF16),
                    jax.ShapeDtypeStruct((slides, width + bank), F32),
                    jax.ShapeDtypeStruct((heads // 2 * LANES, width), BF16),
                ),
                [SMEM, VMEM, VMEM, plane(w3, 0), VMEM, VMEM, VMEM],
                (VMEM, VMEM, VMEM),
                grid=(1,),
                flops=10**9,
                moved=4 * 10**6,
            )(slide_len, tokens, normed, w3, q_gain, w_out, reports)
            for m in range(1, nz):
                got[2 * m + 1] = lax.ppermute(got[2 * m], "sub", swap)
            refs = [got[m] for m in range(blocks)]
            out = call(
                functools.partial(attend_kernel, heads, blocks, slides),
                jax.ShapeDtypeStruct((heads // 2, rows, LANES), BF16),
                [SMEM, SMEM, VMEM] + [ANY] * blocks,
                VMEM,
                [
                    pltpu.VMEM((blocks, full * per, LANES), BF16),
                    pltpu.VMEM((blocks * rows, LANES), BF16),
                    pltpu.VMEM((rows, LANES), F32),
                    pltpu.SMEM((blocks + 1,), I32),
                    pltpu.SMEM((blocks + 1,), I32),
                    pltpu.SemaphoreType.DMA((blocks,)),
                ],
                vmem=6 + (blocks + 2) * full * per * LANES * 2 // MIB,
            )(meta, slide_len, q, *refs)
            return out, tok_sums, wide, rep_got

        return run

    out, tok_sums, wide, rep_got = lax.switch(
        meta[0],
        [branch(caps) for caps in ladder],
        (pack, normed, tokens, w3, q_gain, w_out, reports, meta, slide_len),
    )
    terms, sums = call(
        functools.partial(away_kernel, slides),
        (
            jax.ShapeDtypeStruct((rows, cols if nx == 2 else width), BF16),
            jax.ShapeDtypeStruct((slides, width + bank), F32),
        ),
        [SMEM, VMEM, VMEM, VMEM],
        (VMEM, VMEM),
    )(slide_len, tok_sums, out, wide)
    if nx == 2:
        sums = sums + lax.ppermute(sums, "sub", swap)
        step = 1
        while step < nz:
            sums = sums + lax.ppermute(sums, "ctx", [(i, i ^ step) for i in range(nz)])
            step *= 2
        got = lax.ppermute(terms, "head", swap)
        other = lax.ppermute(sums, "head", swap)
        mixed = call(
            mix_kernel,
            jax.ShapeDtypeStruct((rows, cols), BF16),
            [VMEM] * 4,
            VMEM,
            [pltpu.VMEM((cols // LANES, rows, LANES), F32)],
            flops=10**9,
            moved=4 * 10**6,
        )(tokens, out, wide, got)
        reps = (reports, rep_got)
    else:
        sums = lax.psum(sums, ("ctx", "sub", "head"))
        other = sums
        back = jnp.array([rev(r) for r in range(RES)])
        terms = jnp.transpose(terms.reshape(RES, per, width)[back], (1, 0, 2)).reshape(rows, width)
        proj = lax.psum_scatter(terms, "head", scatter_dimension=1, tiled=True)
        x_cols = lax.dynamic_slice_in_dim(tokens, lax.axis_index("head") * cols, cols, 1)
        mixed = (x_cols.astype(F32) + proj.astype(F32)).astype(BF16)
        reps = (rep_got,)
    similarity, loss = call(
        functools.partial(loss_kernel, nx == 2),
        (jax.ShapeDtypeStruct((slides, bank), F32), jax.ShapeDtypeStruct((slides,), F32)),
        [SMEM, SMEM, SMEM, VMEM, VMEM] + [VMEM] * len(reps),
        (VMEM, VMEM),
    )(slide_len, pairs, log_scale, sums, other, *reps)
    return (mixed, similarity, loss)


def solution(mesh):
    in_specs = (
        P(("groups", "ctx", "sub"), None),
        P(),
        P(None, None, "head"),
        P("head"),
        P("head"),
        P("head", None),
        P(),
        P(),
        P("groups"),
        P(None, "head"),
        P("groups"),
        P(),
    )
    out_specs = (P(("groups", "ctx", "sub"), "head"), P("groups", None), P("groups"))
    return jax.shard_map(run_device, mesh=mesh, in_specs=in_specs, out_specs=out_specs, check_vma=False)
```

time: 300 us -> 60.7 us (0.20)
  matrix products: 115 us -> 0 us
  waiting for transfers between devices: 92.5 us -> 15.5 us
  blocking collectives: 33.4 us -> 0 us
  other arithmetic: 24.9 us -> 0.02 us
  Pallas kernels: 0 us -> 21.1 us
  starting transfers between devices: 0.12 us -> 19 us
  local copies, waits for them, and re-layouts: 16.8 us -> 2.77 us
  between operations: 15.4 us -> 1.45 us
    dot_general x20 -> x0, matrix products: 115 us -> none  [the longest x8 56.3 us: step(): jnp.einsum('qhd,khd->hqk', qn, kb, preferred_element_type=jnp.float32)]
    all_gather x2 -> x0, waiting for transfers between devices: 76.8 us -> none  [the longest x1 39.3 us: per_device(): vpiece = lax.all_gather(vflat, ('ctx', 'sub'), axis=0, tiled=True)]
    psum x2 -> x0, blocking collectives: 33.4 us -> none  [the longest x1 28.4 us: per_device(): sums = lax.psum(partial_sums, ('ctx', 'sub'))]
    pallas_call x0 -> x6, Pallas kernels: none -> 21.1 us  [the longest x1 6.71 us: run(): call(functools.partial(attend_kernel, heads, blocks, slides), jax.ShapeDt...]
    ppermute x0 -> x13, starting transfers between devices: none -> 19 us  [the longest x2 7.52 us: run_device(): sums = sums + lax.ppermute(sums, 'ctx', [(i, i ^ step) for i in range(nz)])]
    unnamed x4 -> x0, waiting for transfers between devices: 15.7 us -> none
    ppermute x0 -> x13, waiting for transfers between devices: none -> 15.5 us  [the longest x3 9.64 us: run(): got[2 * m] = lax.ppermute(pack[:mid if m == 1 else far], 'ctx', ends)]
    add x28 -> x3, other arithmetic: 10 us -> 0.02 us  [the longest x2 0.01 us: run_device(): sums = sums + lax.ppermute(sums, 'ctx', [(i, i ^ step) for i in range(nz)])]
  transfers between devices with their start and end apart: 3 -> 13, of which waited for: 3 -> 6; matrix products, arithmetic and copies ran while one was open for 1% -> 0% of each run, Pallas kernels for 0% -> 21%
where the time goes in v1:
time: 60.7 us; the launch traced here: 60.4 us
  Pallas kernels  21.1 us (35%)
  starting transfers between devices  19 us (31%)
  waiting for transfers between devices  15.5 us (26%)
  local copies, waits for them, and re-layouts  2.77 us (5%)
  between operations  1.45 us (2%)
    ppermute x3, waiting for transfers between devices, run(): got[2 * m] = lax.ppermute(pack[:mid if m == 1 else far], 'ctx', ends)  9.64 us
    ppermute x2, starting transfers between devices, run_device(): sums = sums + lax.ppermute(sums, 'ctx', [(i, i ^ step) for i in range(nz)])  7.52 us
    pallas_call x1, Pallas kernels, run(): call(functools.partial(attend_kernel, heads, blocks, slides), jax.ShapeDt...  6.71 us
    ppermute x3, starting transfers between devices, run(): got[2 * m] = lax.ppermute(pack[:mid if m == 1 else far], 'ctx', ends)  6.58 us
    pallas_call x1, Pallas kernels, run_device(): call(functools.partial(keys_kernel, ladder, heads, nx, classes, slides),...  5.34 us
    pallas_call x1, Pallas kernels, run(): call(functools.partial(queries_kernel, heads, slides, blocks), (jax.Shape...  4.07 us
    ppermute x2, waiting for transfers between devices, run_device(): sums = sums + lax.ppermute(sums, 'ctx', [(i, i ^ step) for i in range(nz)])  3.79 us
    unnamed x26, local copies, waits for them, and re-layouts  2.71 us
  transfers between devices with their start and end apart: 13, of which 6 were waited for; matrix products, arithmetic and copies ran while one was open for 0% of the time, Pallas kernels for 21%

profile of v1, /device:TPU:0, one launch (start us, length us, event | category | flops | bytes accessed | tf_op | source)
XLA Modules:
  0.0 60.4 jit_solution(18082992270995990258)
XLA Ops:
  0.6 0.0 copy-start
  0.6 0.7 %copy-done = f32[768]{0:T(1024)S(1)} copy-done((f32[768]{0:T(1024)S(1)}, f32[768]{0:T(1024)}, u32[]{:S(2)}) %copy-start) | copy-done | bytes 3096
  1.3 0.7 %copy-done.1 = f32[384]{0:T(512)S(1)} copy-done((f32[384]{0:T(512)S(1)}, f32[384]{0:T(512)}, u32[]{:S(2)}) %copy-start.1) | copy-done | bytes 1560
  2.0 0.7 %copy-done.3 = s32[16]{0:T(128)S(1)} copy-done((s32[16]{0:T(128)S(1)}, s32[16]{0:T(128)}, u32[]{:S(2)}) %copy-start.3) | copy-done | bytes 88
  2.7 0.7 %copy-done.4 = s32[16]{0:T(128)S(1)} copy-done((s32[16]{0:T(128)S(1)}, s32[16]{0:T(128)}, u32[]{:S(2)}) %copy-start.4) | copy-done | bytes 88
  3.3 0.0 copy-start.11
  3.3 0.0 copy-start.12
  3.3 5.3 %shard_map.139 = (bf16[4096,128]{1,0:T(8,128)(2,1)S(1)}, bf16[512,768]{1,0:T(8,128)(2,1)S(1)}, s32[36]{0:T(128)S(1)}) custom-call(s32[16]{0:T(128)S(1)} %copy-done.3, s32[16]{0:T(128)S(1)} %copy-done.4, s32[8]{0:T(128)} %len_ref.5, bf16[512,768]{1,0:T(8,128)(2,1)} %x_ref.3, f32[768]{0:T(1024)S(1)} %copy-done, bf16[3,768,384]{2,1,0:T(8,128)(2,1)} %bitcast.3, ...), custom_call_target="tpu_custom_call" | custom-call | flops 1000000 | bytes 1000000 | tf_op jit(solution)/shard_map/pallas_call | solution.py:481
  8.7 0.0 copy-done.5
  8.7 0.0 copy-done.6
  8.7 0.0 copy-done.8
  8.8 0.0 copy-done.9
  8.8 0.0 copy-done.11
  8.8 0.0 copy-start.2
  8.8 29.7 %conditional.1 = (bf16[4,512,128]{2,1,0:T(8,128)(2,1)S(1)}, f32[8,1024]{1,0:T(8,128)S(1)}, bf16[512,768]{1,0:T(8,128)(2,1)S(1)}, bf16[256,384]{1,0:T(8,128)(2,1)}) conditional(s32[]{:T(128)} %bitcast.1, (s32[8]{0:T(128)S(1)}, bf16[512,768]{1,0:T(8,128)(2,1)S(1)}, bf16[512,768]{1,0:T(8,128)(2,1)S(1)}, ...), branch_computations={%region_0.0_spmd, %region_1.0_spmd, %region_2.0_spmd, %region_3.0_... | conditional | flops 1001000000 | bytes 35146912 | solution.py:545
  8.9 3.1 %collective-permute-start.9 = (bf16[1024,128]{1,0:T(8,128)(2,1)S(1)}, bf16[1024,128]{1,0:T(8,128)(2,1)S(1)}, u32[]{:S(2)}, u32[]{:S(2)}) collective-permute-start(bf16[1024,128]{1,0:T(8,128)(2,1)S(1)} %slice.57), channel_id=1, source_target_pairs={{0,4},{4,0},{8,12},{12,8},{1,5},{5,1},{9,13},{13,9},{2,6},{6,2},{1... | collective-permute-start | bytes 786440 | tf_op jit(solution)/shard_map/cond/branch_1_fun/ppermute | solution.py:504
  12.0 0.1 collective-permute-start.8
  12.1 6.2 %collective-permute-done.9.rest_2_ = bf16[1024,128]{1,0:T(8,128)(2,1)S(1)} collective-permute-done((bf16[1024,128]{1,0:T(8,128)(2,1)S(1)}, bf16[1024,128]{1,0:T(8,128)(2,1)S(1)}, u32[]{:S(2)}, u32[]{:S(2)}) %collective-permute-start.9) | collective-permute-done | bytes 262176 | tf_op jit(solution)/shard_map/cond/branch_1_fun/ppermute | solution.py:504
  18.3 0.0 collective-permute-start.10
  18.3 2.8 %collective-permute-start.11 = (bf16[384,128]{1,0:T(8,128)(2,1)S(1)}, bf16[384,128]{1,0:T(8,128)(2,1)S(1)}, u32[]{:S(2)}, u32[]{:S(2)}) collective-permute-start(bf16[384,128]{1,0:T(8,128)(2,1)S(1)} %slice.58), channel_id=1, source_target_pairs={{0,8},{4,12},{8,0},{12,4},{1,9},{5,13},{9,1},{13,5},{2,10},{6,14},... | collective-permute-start | bytes 294920 | tf_op jit(solution)/shard_map/cond/branch_1_fun/ppermute | solution.py:504
  21.1 0.7 %collective-permute-start.13 = (bf16[384,128]{1,0:T(8,128)(2,1)S(1)}, bf16[384,128]{1,0:T(8,128)(2,1)S(1)}, u32[]{:S(2)}, u32[]{:S(2)}) collective-permute-start(bf16[384,128]{1,0:T(8,128)(2,1)S(1)} %slice.58), channel_id=1, source_target_pairs={{4,8},{8,4},{5,9},{9,5},{6,10},{10,6},{7,11},{11,7},{20,24},{24,20... | collective-permute-start | bytes 294920 | tf_op jit(solution)/shard_map/cond/branch_1_fun/ppermute | solution.py:504
  21.8 1.5 %collective-permute-start.15 = (bf16[256,384]{1,0:T(8,128)(2,1)S(1)}, bf16[256,384]{1,0:T(8,128)(2,1)}, u32[]{:S(2)}, u32[]{:S(2)}) collective-permute-start(bf16[256,384]{1,0:T(8,128)(2,1)S(1)} %get-tuple-element.181.rep_ref), channel_id=1, source_target_pairs={{0,2},{2,0},{1,3},{3,1},{4,6},{6,4},{5,7},{7,5},{8,10},{10,8},{9,1... | collective-permute-start | bytes 589832 | tf_op jit(solution)/shard_map/cond/branch_1_fun/ppermute | solution.py:507
  23.2 3.4 %collective-permute-done.11.rest_4_ = bf16[384,128]{1,0:T(8,128)(2,1)S(1)} collective-permute-done((bf16[384,128]{1,0:T(8,128)(2,1)S(1)}, bf16[384,128]{1,0:T(8,128)(2,1)S(1)}, u32[]{:S(2)}, u32[]{:S(2)}) %collective-permute-start.11) | collective-permute-done | bytes 98336 | tf_op jit(solution)/shard_map/cond/branch_1_fun/ppermute | solution.py:504
  26.7 0.0 collective-permute-start.12
  26.7 0.0 collective-permute-done.13.rest_6_
  26.7 0.5 collective-permute-start.14
  27.2 4.1 %branch_1_fun.2 = (bf16[8,512,128]{2,1,0:T(8,128)(2,1)S(1)}, f32[8,1024]{1,0:T(8,128)S(1)}, bf16[512,768]{1,0:T(8,128)(2,1)S(1)}) custom-call(s32[8]{0:T(128)S(1)} %get-tuple-element.175.len_ref, bf16[512,768]{1,0:T(8,128)(2,1)S(1)} %get-tuple-element.176.x_ref, bf16[512,768]{1,0:T(8,128)(2,1)S(1)} %get-tuple-element.177.normed_ref, ...), custom_call_target="tpu_custom_call" | custom-call | flops 1000000000 | bytes 4000000 | tf_op jit(solution)/shard_map/cond/branch_1_fun/pallas_call | solution.py:510
  31.3 0.0 collective-permute-done.12.rest_5_
  31.3 0.0 collective-permute-done.14.rest_7_
  31.3 0.0 collective-permute-done.10.rest_3_
  31.3 0.0 collective-permute-done.8.rest_1_
  31.3 6.7 %branch_1_fun.3 = bf16[4,512,128]{2,1,0:T(8,128)(2,1)S(1)} custom-call(s32[36]{0:T(128)S(1)} %get-tuple-element.174.meta_ref, s32[8]{0:T(128)S(1)} %get-tuple-element.175.len_ref, bf16[8,512,128]{2,1,0:T(8,128)(2,1)S(1)} %get-tuple-element.182.q_ref, bf16[4096,128]{1,0:T(8,128)(2,1)S(1)} %get-tuple-element.183.rest_0_, ...), custom_call_target="tpu_custom_call" | custom-call | flops 1000000 | bytes 1000000 | tf_op jit(solution)/shard_map/cond/branch_1_fun/pallas_call | solution.py:526
  38.0 0.0 collective-permute-done.15
  38.5 0.0 copy-start.10
  38.5 0.0 copy-start.7
  38.5 1.6 %shard_map.140 = (bf16[512,384]{1,0:T(8,128)(2,1)S(1)}, f32[8,1024]{1,0:T(8,128)S(1)}) custom-call(s32[8]{0:T(128)S(1)} %copy-done.11, f32[8,1024]{1,0:T(8,128)S(1)} %get-tuple-element.289.tok_sums_ref, bf16[4,512,128]{2,1,0:T(8,128)(2,1)S(1)} %get-tuple-element.287.out_ref, bf16[512,768]{1,0:T(8,128)(2,1)S(1)} %get-tuple-element.288.wide_ref), custom_call_target="tpu_custom_call" | custom-call | flops 1000000 | bytes 1000000 | tf_op jit(solution)/shard_map/pallas_call | solution.py:550
  40.1 0.2 collective-permute-start.72
  40.3 0.4 collective-permute-start.73
  40.7 0.9 %collective-permute-done.73 = f32[8,1024]{1,0:T(8,128)S(1)} collective-permute-done((f32[8,1024]{1,0:T(8,128)S(1)}, f32[8,1024]{1,0:T(8,128)S(1)}, u32[]{:S(2)}, u32[]{:S(2)}) %collective-permute-start.73) | collective-permute-done | bytes 32800 | tf_op jit(solution)/shard_map/ppermute | solution.py:560
  41.5 3.6 %collective-permute-start.74 = (f32[8,1024]{1,0:T(8,128)S(1)}, f32[8,1024]{1,0:T(8,128)S(1)}, u32[]{:S(2)}, u32[]{:S(2)}) collective-permute-start(f32[8,1024]{1,0:T(8,128)S(1)} %add.9), channel_id=1, source_target_pairs={{0,4},{4,0},{8,12},{12,8},{1,5},{5,1},{9,13},{13,9},{2,6},{6,2},{1... | collective-permute-start | bytes 98312 | tf_op jit(solution)/shard_map/ppermute | solution.py:563
  45.1 1.9 %collective-permute-done.74 = f32[8,1024]{1,0:T(8,128)S(1)} collective-permute-done((f32[8,1024]{1,0:T(8,128)S(1)}, f32[8,1024]{1,0:T(8,128)S(1)}, u32[]{:S(2)}, u32[]{:S(2)}) %collective-permute-start.74) | collective-permute-done | bytes 32800 | tf_op jit(solution)/shard_map/ppermute | solution.py:563
  47.0 3.9 %collective-permute-start.75 = (f32[8,1024]{1,0:T(8,128)S(1)}, f32[8,1024]{1,0:T(8,128)S(1)}, u32[]{:S(2)}, u32[]{:S(2)}) collective-permute-start(f32[8,1024]{1,0:T(8,128)S(1)} %add.10), channel_id=1, source_target_pairs={{0,8},{4,12},{8,0},{12,4},{1,9},{5,13},{9,1},{13,5},{2,10},{6,14},... | collective-permute-start | bytes 98312 | tf_op jit(solution)/shard_map/ppermute | solution.py:563
  51.0 1.9 %collective-permute-done.75 = f32[8,1024]{1,0:T(8,128)S(1)} collective-permute-done((f32[8,1024]{1,0:T(8,128)S(1)}, f32[8,1024]{1,0:T(8,128)S(1)}, u32[]{:S(2)}, u32[]{:S(2)}) %collective-permute-start.75) | collective-permute-done | bytes 32800 | tf_op jit(solution)/shard_map/ppermute | solution.py:563
  52.9 2.3 %collective-permute-start.76 = (f32[8,1024]{1,0:T(8,128)S(1)}, f32[8,1024]{1,0:T(8,128)S(1)}, u32[]{:S(2)}, u32[]{:S(2)}) collective-permute-start(f32[8,1024]{1,0:T(8,128)S(1)} %add.11.sums_ref), channel_id=1, source_target_pairs={{0,2},{2,0},{1,3},{3,1},{4,6},{6,4},{5,7},{7,5},{8,10},{10,8},{9,1... | collective-permute-start | bytes 98312 | tf_op jit(solution)/shard_map/ppermute | solution.py:566
  55.8 1.2 %collective-permute-done.76.other_ref = f32[8,1024]{1,0:T(8,128)S(1)} collective-permute-done((f32[8,1024]{1,0:T(8,128)S(1)}, f32[8,1024]{1,0:T(8,128)S(1)}, u32[]{:S(2)}, u32[]{:S(2)}) %collective-permute-start.76) | collective-permute-done | bytes 32800 | tf_op jit(solution)/shard_map/ppermute | solution.py:566
  57.1 1.8 %shard_map.142 = (f32[8,256]{1,0:T(8,128)}, f32[8]{0:T(128)}) custom-call(s32[8]{0:T(128)S(1)} %copy-done.11, s32[8]{0:T(128)S(1)} %copy-done.2, f32[1]{0:T(128)S(6)} %copy.51.scale_ref, f32[8,1024]{1,0:T(8,128)S(1)} %add.11.sums_ref, f32[8,1024]{1,0:T(8,128)S(1)} %collective-permute-done.76.other_ref, bf16[256,384]{1,0:T(8,128)(2,1)S(1)} %copy-done.10, ...), custom_call_target="tpu_custom_call" | custom-call | flops 1000000 | bytes 1000000 | tf_op jit(solution)/shard_map/pallas_call | solution.py:586
  58.8 0.0 collective-permute-done.72.got_ref
  58.9 1.6 %shard_map.141 = bf16[512,384]{1,0:T(8,128)(2,1)} custom-call(bf16[512,768]{1,0:T(8,128)(2,1)S(1)} %copy-done.7, bf16[4,512,128]{2,1,0:T(8,128)(2,1)S(1)} %get-tuple-element.287.out_ref, bf16[512,768]{1,0:T(8,128)(2,1)S(1)} %get-tuple-element.288.wide_ref, bf16[512,384]{1,0:T(8,128)(2,1)S(1)} %collective-permute-done.72.got_ref), custom_call_target="tpu_custom_call" | custom-call | flops 1000000000 | bytes 4000000 | tf_op jit(solution)/shard_map/pallas_call | solution.py:567
  (17 shorter events, 0.1 us)
Async XLA Ops:
  0.6 0.7 %copy-start = (f32[768]{0:T(1024)S(1)}, f32[768]{0:T(1024)}, u32[]{:S(2)}) copy-start(f32[768]{0:T(1024)} %ng_ref.1) | copy-start | bytes 9220
  1.3 0.7 %copy-start.1 = (f32[384]{0:T(512)S(1)}, f32[384]{0:T(512)}, u32[]{:S(2)}) copy-start(f32[384]{0:T(512)} %kg_ref.1) | copy-start | bytes 4612
  2.0 0.7 %copy-start.3 = (s32[16]{0:T(128)S(1)}, s32[16]{0:T(128)}, u32[]{:S(2)}) copy-start(s32[16]{0:T(128)} %seg_ref.1) | copy-start | bytes 196
  2.7 0.7 %copy-start.4 = (s32[16]{0:T(128)S(1)}, s32[16]{0:T(128)}, u32[]{:S(2)}) copy-start(s32[16]{0:T(128)} %dil_ref.1) | copy-start | bytes 196
  3.3 5.4 %copy-start.5 = (bf16[768,3,384]{2,0,1:T(8,128)(2,1)S(1)}, bf16[768,3,384]{2,0,1:T(8,128)(2,1)}, u32[]{:S(2)}) copy-start(bf16[768,3,384]{2,0,1:T(8,128)(2,1)} %param.23) | copy-start | bytes 5308420
  3.3 5.4 %copy-start.6 = (bf16[512,768]{1,0:T(8,128)(2,1)S(1)}, bf16[512,768]{1,0:T(8,128)(2,1)}, u32[]{:S(2)}) copy-start(bf16[512,768]{1,0:T(8,128)(2,1)} %x_ref.3) | copy-start | bytes 2359300
  3.3 5.4 %copy-start.8 = (bf16[384,768]{1,0:T(8,128)(2,1)S(1)}, bf16[384,768]{1,0:T(8,128)(2,1)}, u32[]{:S(2)}) copy-start(bf16[384,768]{1,0:T(8,128)(2,1)} %param.26) | copy-start | bytes 1769476
  3.3 5.4 %copy-start.9 = (bf16[256,384]{1,0:T(8,128)(2,1)S(1)}, bf16[256,384]{1,0:T(8,128)(2,1)}, u32[]{:S(2)}) copy-start(bf16[256,384]{1,0:T(8,128)(2,1)} %rest_0_.1) | copy-start | bytes 589828
  3.3 5.4 %copy-start.11 = (s32[8]{0:T(128)S(1)}, s32[8]{0:T(128)}, u32[]{:S(2)}) copy-start(s32[8]{0:T(128)} %len_ref.5) | copy-start | bytes 100
  3.3 5.4 %copy-start.12 = (f32[384]{0:T(512)S(1)}, f32[384]{0:T(512)}, u32[]{:S(2)}) copy-start(f32[384]{0:T(512)} %param.24) | copy-start | bytes 4612
  8.8 48.3 %copy-start.2 = (s32[8]{0:T(128)S(1)}, s32[8]{0:T(128)}, u32[]{:S(2)}) copy-start(s32[8]{0:T(128)} %pairs_ref.1) | copy-start | bytes 100
  8.9 9.4 %collective-permute-start.9 = (bf16[1024,128]{1,0:T(8,128)(2,1)S(1)}, bf16[1024,128]{1,0:T(8,128)(2,1)S(1)}, u32[]{:S(2)}, u32[]{:S(2)}) collective-permute-start(bf16[1024,128]{1,0:T(8,128)(2,1)S(1)} %slice.57), channel_id=1, source_target_pairs={{0,4},{4,0},{8,12},{12,8},{1,5},{5,1},{9,13},{13,9},{2,6},{6,2},{1... | collective-permute-start | bytes 786440 | tf_op jit(solution)/shard_map/cond/branch_1_fun/ppermute | solution.py:504
  12.0 19.3 %collective-permute-start.8 = (bf16[2048,128]{1,0:T(8,128)(2,1)S(1)}, bf16[2048,128]{1,0:T(8,128)(2,1)S(1)}, u32[]{:S(2)}, u32[]{:S(2)}) collective-permute-start(bf16[2048,128]{1,0:T(8,128)(2,1)S(1)} %slice.52), channel_id=1, source_target_pairs={{0,1},{1,0},{2,3},{3,2},{4,5},{5,4},{6,7},{7,6},{8,9},{9,8},{10,11... | collective-permute-start | bytes 1572872 | tf_op jit(solution)/shard_map/cond/branch_1_fun/ppermute | solution.py:505
  18.3 13.0 %collective-permute-start.10 = (bf16[1024,128]{1,0:T(8,128)(2,1)S(1)}, bf16[1024,128]{1,0:T(8,128)(2,1)S(1)}, u32[]{:S(2)}, u32[]{:S(2)}) collective-permute-start(bf16[1024,128]{1,0:T(8,128)(2,1)S(1)} %collective-permute-done.9.rest_2_), channel_id=1, source_target_pairs={{0,1},{1,0},{2,3},{3,2},{4,5},{5,4},{6,7},{7,6},{8,9},{9,8},{10,11... | collective-permute-start | bytes 786440 | tf_op jit(solution)/shard_map/cond/branch_1_fun/ppermute | solution.py:524
  18.3 8.4 %collective-permute-start.11 = (bf16[384,128]{1,0:T(8,128)(2,1)S(1)}, bf16[384,128]{1,0:T(8,128)(2,1)S(1)}, u32[]{:S(2)}, u32[]{:S(2)}) collective-permute-start(bf16[384,128]{1,0:T(8,128)(2,1)S(1)} %slice.58), channel_id=1, source_target_pairs={{0,8},{4,12},{8,0},{12,4},{1,9},{5,13},{9,1},{13,5},{2,10},{6,14},... | collective-permute-start | bytes 294920 | tf_op jit(solution)/shard_map/cond/branch_1_fun/ppermute | solution.py:504
  21.1 5.6 %collective-permute-start.13 = (bf16[384,128]{1,0:T(8,128)(2,1)S(1)}, bf16[384,128]{1,0:T(8,128)(2,1)S(1)}, u32[]{:S(2)}, u32[]{:S(2)}) collective-permute-start(bf16[384,128]{1,0:T(8,128)(2,1)S(1)} %slice.58), channel_id=1, source_target_pairs={{4,8},{8,4},{5,9},{9,5},{6,10},{10,6},{7,11},{11,7},{20,24},{24,20... | collective-permute-start | bytes 294920 | tf_op jit(solution)/shard_map/cond/branch_1_fun/ppermute | solution.py:504
  21.8 16.2 %collective-permute-start.15 = (bf16[256,384]{1,0:T(8,128)(2,1)S(1)}, bf16[256,384]{1,0:T(8,128)(2,1)}, u32[]{:S(2)}, u32[]{:S(2)}) collective-permute-start(bf16[256,384]{1,0:T(8,128)(2,1)S(1)} %get-tuple-element.181.rep_ref), channel_id=1, source_target_pairs={{0,2},{2,0},{1,3},{3,1},{4,6},{6,4},{5,7},{7,5},{8,10},{10,8},{9,1... | collective-permute-start | bytes 589832 | tf_op jit(solution)/shard_map/cond/branch_1_fun/ppermute | solution.py:507
  26.7 4.6 %collective-permute-start.12 = (bf16[384,128]{1,0:T(8,128)(2,1)S(1)}, bf16[384,128]{1,0:T(8,128)(2,1)S(1)}, u32[]{:S(2)}, u32[]{:S(2)}) collective-permute-start(bf16[384,128]{1,0:T(8,128)(2,1)S(1)} %collective-permute-done.11.rest_4_), channel_id=1, source_target_pairs={{0,1},{1,0},{2,3},{3,2},{4,5},{5,4},{6,7},{7,6},{8,9},{9,8},{10,11... | collective-permute-start | bytes 294920 | tf_op jit(solution)/shard_map/cond/branch_1_fun/ppermute | solution.py:524
  26.7 4.6 %collective-permute-start.14 = (bf16[384,128]{1,0:T(8,128)(2,1)S(1)}, bf16[384,128]{1,0:T(8,128)(2,1)S(1)}, u32[]{:S(2)}, u32[]{:S(2)}) collective-permute-start(bf16[384,128]{1,0:T(8,128)(2,1)S(1)} %collective-permute-done.13.rest_6_), channel_id=1, source_target_pairs={{0,1},{1,0},{2,3},{3,2},{4,5},{5,4},{6,7},{7,6},{8,9},{9,8},{10,11... | collective-permute-start | bytes 294920 | tf_op jit(solution)/shard_map/cond/branch_1_fun/ppermute | solution.py:524
  38.5 18.6 %copy-start.10 = (bf16[256,384]{1,0:T(8,128)(2,1)S(1)}, bf16[256,384]{1,0:T(8,128)(2,1)}, u32[]{:S(2)}) copy-start(bf16[256,384]{1,0:T(8,128)(2,1)} %rest_0_.1) | copy-start | bytes 589828
  38.5 20.4 %copy-start.7 = (bf16[512,768]{1,0:T(8,128)(2,1)S(1)}, bf16[512,768]{1,0:T(8,128)(2,1)}, u32[]{:S(2)}) copy-start(bf16[512,768]{1,0:T(8,128)(2,1)} %x_ref.3) | copy-start | bytes 2359300
  40.1 18.8 %collective-permute-start.72 = (bf16[512,384]{1,0:T(8,128)(2,1)S(1)}, bf16[512,384]{1,0:T(8,128)(2,1)S(1)}, u32[]{:S(2)}, u32[]{:S(2)}) collective-permute-start(bf16[512,384]{1,0:T(8,128)(2,1)S(1)} %get-tuple-element.290), channel_id=1, source_target_pairs={{0,2},{2,0},{1,3},{3,1},{4,6},{6,4},{5,7},{7,5},{8,10},{10,8},{9,1... | collective-permute-start | bytes 1179656 | tf_op jit(solution)/shard_map/ppermute | solution.py:565
  40.3 1.3 %collective-permute-start.73 = (f32[8,1024]{1,0:T(8,128)S(1)}, f32[8,1024]{1,0:T(8,128)S(1)}, u32[]{:S(2)}, u32[]{:S(2)}) collective-permute-start(f32[8,1024]{1,0:T(8,128)S(1)} %get-tuple-element.291), channel_id=1, source_target_pairs={{0,1},{1,0},{2,3},{3,2},{4,5},{5,4},{6,7},{7,6},{8,9},{9,8},{10,11... | collective-permute-start | bytes 98312 | tf_op jit(solution)/shard_map/ppermute | solution.py:560
  41.5 5.5 %collective-permute-start.74 = (f32[8,1024]{1,0:T(8,128)S(1)}, f32[8,1024]{1,0:T(8,128)S(1)}, u32[]{:S(2)}, u32[]{:S(2)}) collective-permute-start(f32[8,1024]{1,0:T(8,128)S(1)} %add.9), channel_id=1, source_target_pairs={{0,4},{4,0},{8,12},{12,8},{1,5},{5,1},{9,13},{13,9},{2,6},{6,2},{1... | collective-permute-start | bytes 98312 | tf_op jit(solution)/shard_map/ppermute | solution.py:563
  47.0 5.8 %collective-permute-start.75 = (f32[8,1024]{1,0:T(8,128)S(1)}, f32[8,1024]{1,0:T(8,128)S(1)}, u32[]{:S(2)}, u32[]{:S(2)}) collective-permute-start(f32[8,1024]{1,0:T(8,128)S(1)} %add.10), channel_id=1, source_target_pairs={{0,8},{4,12},{8,0},{12,4},{1,9},{5,13},{9,1},{13,5},{2,10},{6,14},... | collective-permute-start | bytes 98312 | tf_op jit(solution)/shard_map/ppermute | solution.py:563
  52.9 4.2 %collective-permute-start.76 = (f32[8,1024]{1,0:T(8,128)S(1)}, f32[8,1024]{1,0:T(8,128)S(1)}, u32[]{:S(2)}, u32[]{:S(2)}) collective-permute-start(f32[8,1024]{1,0:T(8,128)S(1)} %add.11.sums_ref), channel_id=1, source_target_pairs={{0,2},{2,0},{1,3},{3,1},{4,6},{6,4},{5,7},{7,5},{8,10},{10,8},{9,1... | collective-permute-start | bytes 98312 | tf_op jit(solution)/shard_map/ppermute | solution.py:566

commit v2 on v1

--- a/solution.py
+++ b/solution.py
@@ -104,7 +104,11 @@
         first = jnp.where(lane >= h * HEAD_DIM, h * HEAD_DIM, first)
     row = lax.broadcasted_iota(I32, (feat, feat), 0)
     same = jnp.where((row >= first) & (row < first + HEAD_DIM), 1.0, 0.0).astype(BF16)
-    return lax.rsqrt((dot(high, same) + dot(low, same)) * (1.0 / HEAD_DIM) + 1e-06)
+    if feat % LANES:
+        total = dot(high, same) + dot(low, same)
+    else:
+        total = dot(jnp.concatenate([high, low], axis=1), jnp.concatenate([same, same], axis=0))
+    return lax.rsqrt(total * (1.0 / HEAD_DIM) + 1e-06)
 
 
 def span(pair, feat):
@@ -126,10 +130,28 @@
 
 
 def keys_kernel(
-    ladder, heads, parts, classes, slides, seg_ref, dil_ref, len_ref, x_ref, ng_ref, wk_ref, wv_ref, kg_ref,
-    pack_ref, normed_ref, meta_ref, xs_ref, kv_ref,
+    ladder, heads, parts, classes, slides, seg_hbm, dil_hbm, len_hbm, x_hbm, ng_hbm, w_hbm, kg_hbm,
+    pack_ref, normed_ref, meta_ref, xs_ref, kv_ref, x_ref, kv_w_ref, seg_ref, dil_ref, len_ref, ng_ref, kg_ref, sem,
 ):
     rows, width = x_ref.shape
+    feat = heads * HEAD_DIM
+    joined = len(kv_w_ref.shape) == 2
+    k_w_ref = kv_w_ref.at[:, pl.ds(0, feat)] if joined else kv_w_ref.at[0]
+    v_w_ref = kv_w_ref.at[:, pl.ds(feat, feat)] if joined else kv_w_ref.at[1]
+    small = []
+    for i, (source, target) in enumerate(
+        ((seg_hbm, seg_ref), (dil_hbm, dil_ref), (len_hbm, len_ref), (ng_hbm, ng_ref), (kg_hbm, kg_ref))
+    ):
+        small.append(pltpu.make_async_copy(source, target, sem.at[3 + i]))
+        small[-1].start()
+    x_copy = pltpu.make_async_copy(x_hbm, x_ref, sem.at[0])
+    x_copy.start()
+    k_copy = pltpu.make_async_copy(w_hbm.at[1], k_w_ref, sem.at[1])
+    k_copy.start()
+    v_copy = pltpu.make_async_copy(w_hbm.at[2], v_w_ref, sem.at[2])
+    v_copy.start()
+    for copy in small:
+        copy.wait()
     feat = heads * HEAD_DIM
     per = rows // RES
     base = lax.axis_index("head") * heads
@@ -169,6 +191,7 @@
         meta_ref[at + OFFSET] = total * per
         meta_ref[at + REACH] = local_seg[h] // rows
 
+    x_copy.wait()
     x = x_ref[...].astype(F32)
     mean_sq = jnp.mean(x * x, axis=-1, keepdims=True)
     normal = x * lax.rsqrt(mean_sq + 1e-06) * ng_ref[...].reshape(1, width)
@@ -179,14 +202,24 @@
             at = rev(r) * per
             normed_ref[at : at + per, lanes] = xs_ref[c, pl.ds(r, per, stride=RES), :].astype(BF16)
     normed = normed_ref[...]
-    keys = dot(normed, wk_ref[0])
-    vals = dot(normed, wv_ref[0]).astype(BF16)
+    k_copy.wait()
+    v_copy.wait()
+    if joined:
+        keys_vals = dot(normed, kv_w_ref[...])
+        keys, vals = keys_vals[:, :feat], keys_vals[:, feat:].astype(BF16)
+    else:
+        keys = dot(normed, kv_w_ref[0])
+        vals = dot(normed, kv_w_ref[1]).astype(BF16)
     kn = (keys * head_scale(keys, feat) * kg_ref[...].reshape(1, feat)).astype(BF16)
     extra = slide_tiles(len_ref, rows, my_start, slides, 1.0, 0.0, -FAR)
     for pair in range(heads // 2):
         first, size = span(pair, feat)
-        both = dot(kn[:, first : first + size], selector(size, first, 2 * pair, K_AT))
-        both = both + dot(vals[:, first : first + size], selector(size, first, 2 * pair, V_AT))
+        mine = slice(first, first + size)
+        to_k, to_v = (selector(size, first, 2 * pair, at) for at in (K_AT, V_AT))
+        if feat % LANES:
+            both = dot(kn[:, mine], to_k) + dot(vals[:, mine], to_v)
+        else:
+            both = dot(jnp.concatenate([kn[:, mine], vals[:, mine]], axis=1), jnp.concatenate([to_k, to_v], axis=0))
         for side in range(2):
             h = 2 * pair + side
             kv_ref[h] = (both[:, side * LANES : (side + 1) * LANES] + extra[side]).astype(BF16)
@@ -245,16 +278,23 @@
         wide_ref[at : at + HEAD_DIM, :] = w_out_ref[h * HEAD_DIM : (h + 1) * HEAD_DIM, :]
 
 
-def attend_kernel(heads, blocks, slides, meta_ref, len_ref, q_ref, *rest):
-    kv_refs = rest[:blocks]
-    out_ref, kvs_ref, keys_ref, acc_ref, list_ref, before_ref, sem = rest[blocks:]
+def attend_kernel(heads, blocks, begin, slides, meta_ref, len_ref, q_ref, *rest):
+    stop = 2 if begin == 0 else blocks
+    if begin > 0:
+        out_in_ref, acc_in_ref, *rest = rest
+    kv_refs, rest = rest[: stop - begin], rest[stop - begin :]
+    if begin > 0:
+        out_ref, *rest = rest
+    else:
+        out_ref, acc_out_ref, *rest = rest
+    kvs_ref, keys_ref, acc_ref, list_ref, before_ref, sem = rest
     rows = q_ref.shape[1]
     per = rows // RES
     me = lax.axis_index(("ctx", "sub"))
     copies = []
-    for m in range(blocks):
-        size = kv_refs[m].shape[0]
-        copies.append(pltpu.make_async_copy(kv_refs[m], kvs_ref.at[m, pl.ds(0, size), :], sem.at[m]))
+    for i, kv_ref in enumerate(kv_refs):
+        size = kv_ref.shape[0]
+        copies.append(pltpu.make_async_copy(kv_ref, kvs_ref.at[i, pl.ds(0, size), :], sem.at[i]))
         copies[-1].start()
     low = jnp.int32(0)
     high = jnp.int32(rows * blocks)
@@ -264,13 +304,13 @@
         low = jnp.where(end <= me * rows, jnp.maximum(low, end), low)
         high = jnp.where(end >= (me + 1) * rows, jnp.minimum(high, end), high)
     count = jnp.int32(0)
-    for m in range(blocks):
+    for i, m in enumerate(range(begin, stop)):
         other = jnp.bitwise_xor(me, m) * rows
-        before_ref[m] = count
-        list_ref[count] = jnp.int32(m)
+        before_ref[i] = count
+        list_ref[count] = jnp.int32(i)
         count = count + ((other < high) & (other + rows > low)).astype(I32)
-    before_ref[blocks] = count
-    out_ref[...] = jnp.zeros_like(out_ref)
+    before_ref[stop - begin] = count
+    out_ref[...] = jnp.zeros_like(out_ref) if begin == 0 else out_in_ref[...]
     lane = lax.broadcasted_iota(I32, (1, LANES), 1)
     outside = jnp.zeros((1, LANES), jnp.bool_)
     for side in range(2):
@@ -285,13 +325,13 @@
         units = meta_ref[entry + UNITS]
         first = meta_ref[entry + FIRST]
         off = meta_ref[entry + OFFSET]
-        some = before_ref[meta_ref[entry + REACH]]
+        some = before_ref[jnp.clip(meta_ref[entry + REACH], begin, stop) - begin]
         pair = h >> 1
         side = h & 1
 
         def attend(u, steps):
             size = u * per
-            tile = min(size * 8, rows)
+            tile = min(size * min(8, pl.next_power_of_2(stop - begin)), rows)
             group = tile // size
             parts = some * steps
             tiles = (parts + (group - 1)) >> (group.bit_length() - 1)
@@ -317,7 +357,7 @@
             def q_step(i, carry):
                 here = pl.ds(pl.multiple_of(first + i * size, per), size)
                 q = q_ref[h, here, :]
-                acc_ref[0:size, :] = jnp.zeros((size, LANES), F32)
+                acc_ref[0:size, :] = jnp.zeros((size, LANES), F32) if begin == 0 else acc_in_ref[h, here, :]
 
                 def k_step(t, carry):
                     kv = keys_ref[pl.ds(pl.multiple_of(t * tile, tile), tile), :]
@@ -327,6 +367,8 @@
 
                 lax.fori_loop(0, tiles, k_step, 0)
                 acc = acc_ref[0:size, :]
+                if begin == 0:
+                    acc_out_ref[h, here, :] = acc
                 total = acc[:, ONE_AT : ONE_AT + 1]
                 safe = jnp.where(total > 0, total, 1.0)
                 res = jnp.where(total > 0, acc / safe, 0.0).astype(BF16)
@@ -336,8 +378,8 @@
             lax.fori_loop(0, steps, q_step, 0)
 
         for u in (1, 2, 4):
-            pl.when(units == u)(functools.partial(attend, u, jnp.int32(1)))
-        pl.when(units >= 8)(functools.partial(attend, 8, units >> 3))
+            pl.when((units == u) & (some > 0))(functools.partial(attend, u, jnp.int32(1)))
+        pl.when((units >= 8) & (some > 0))(functools.partial(attend, 8, units >> 3))
         return carry
 
     lax.fori_loop(0, heads, head_step, 0)
@@ -373,20 +415,31 @@
     terms_ref[...] = dot(out, wide_ref[:, columns]).astype(BF16)
 
 
-def mix_kernel(x_ref, out_ref, wide_ref, got_ref, mixed_ref, p_ref):
-    pairs, rows, _ = out_ref.shape
+def unpermute(values, p_ref):
+    rows = values.shape[0]
     per = rows // RES
-    cols = got_ref.shape[1]
+    for c in range(values.shape[1] // LANES):
+        for r in range(RES):
+            at = rev(r) * per
+            p_ref[c, pl.ds(r, per, stride=RES), :] = values[at : at + per, c * LANES : (c + 1) * LANES]
+
+
+def own_kernel(x_ref, out_ref, wide_ref, y_ref, p_ref):
+    pairs = out_ref.shape[0]
+    cols = y_ref.shape[1]
     mine = pl.multiple_of(lax.axis_index("head") * cols, LANES)
     out = jnp.concatenate([out_ref[pair] for pair in range(pairs)], axis=1)
-    acc = got_ref[...].astype(F32) + dot(out, wide_ref[:, pl.ds(mine, cols)])
+    unpermute(dot(out, wide_ref[:, pl.ds(mine, cols)]), p_ref)
     for c in range(cols // LANES):
+        x = x_ref[:, pl.ds(pl.multiple_of(mine + c * LANES, LANES), LANES)]
+        y_ref[:, c * LANES : (c + 1) * LANES] = x.astype(F32) + p_ref[c]
+
+
+def mix_kernel(y_ref, got_ref, mixed_ref, p_ref):
+    unpermute(got_ref[...].astype(F32), p_ref)
+    for c in range(y_ref.shape[1] // LANES):
         lanes = slice(c * LANES, (c + 1) * LANES)
-        for r in range(RES):
-            at = rev(r) * per
-            p_ref[c, pl.ds(r, per, stride=RES), :] = acc[at : at + per, lanes]
-        x = x_ref[:, pl.ds(pl.multiple_of(mine + c * LANES, LANES), LANES)]
-        mixed_ref[:, lanes] = (x.astype(F32) + p_ref[c]).astype(BF16)
+        mixed_ref[:, lanes] = (y_ref[:, lanes] + p_ref[c]).astype(BF16)
 
 
 def loss_kernel(swapped, len_ref, pairs_ref, scale_ref, sums_ref, other_ref, *rest):
@@ -436,6 +489,7 @@
 SMEM = pl.BlockSpec(memory_space=pltpu.SMEM)
 VMEM = pl.BlockSpec(memory_space=pltpu.VMEM)
 ANY = pl.BlockSpec(memory_space=pl.ANY)
+HBM = pl.BlockSpec(memory_space=pltpu.HBM)
 
 
 def call(kernel, out_shape, in_specs, out_specs, scratch=(), grid=(), vmem=16, flops=1000000, moved=1000000):
@@ -452,7 +506,7 @@
 
 
 def ladder_of(full):
-    steps = ((64, 24, 8), (64, 32, 12), (64, 24, 16), (64, 40, 16), (64, 32, 24), (96, 48, 24), (96, 48, 32), (96, 64, 40))
+    steps = ((96, 38, 18), (96, 42, 21), (96, 50, 25), (96, 58, 29), (96, 68, 34), (96, 82, 41), (96, 82, 58))
     fitting = tuple(step for step in steps if step[0] < full)
     return fitting + ((full, full, full),)
 
@@ -485,11 +539,21 @@
             jax.ShapeDtypeStruct((rows, width), BF16),
             jax.ShapeDtypeStruct((HEAD_AT + heads * FIELDS,), I32),
         ),
-        [SMEM, SMEM, SMEM, VMEM, VMEM, plane(w3, 1), plane(w3, 2), VMEM],
+        [HBM] * 7,
         (VMEM, VMEM, SMEM),
-        [pltpu.VMEM((width // LANES, rows, LANES), F32), pltpu.VMEM((heads, rows, LANES), BF16)],
-        grid=(1,),
-    )(seg_len, dilation, slide_len, tokens, norm_gain, w3, w3, k_gain)
+        [
+            pltpu.VMEM((width // LANES, rows, LANES), F32),
+            pltpu.VMEM((heads, rows, LANES), BF16),
+            pltpu.VMEM((rows, width), BF16),
+            pltpu.VMEM((2, width, feat) if feat % LANES else (width, 2 * feat), BF16),
+            pltpu.SMEM(seg_len.shape, I32),
+            pltpu.SMEM(dilation.shape, I32),
+            pltpu.SMEM(slide_len.shape, I32),
+            pltpu.VMEM((width,), F32),
+            pltpu.VMEM((feat,), F32),
+            pltpu.SemaphoreType.DMA((8,)),
+        ],
+    )(*(pltpu.with_memory_space_constraint(a, pltpu.HBM) for a in (seg_len, dilation, slide_len, tokens, norm_gain, w3, k_gain)))
 
     bank = reports.shape[0]
 
@@ -520,24 +584,37 @@
                 flops=10**9,
                 moved=4 * 10**6,
             )(slide_len, tokens, normed, w3, q_gain, w_out, reports)
+
+            def scratch(count):
+                return [
+                    pltpu.VMEM((count, full * per, LANES), BF16),
+                    pltpu.VMEM((pl.next_power_of_2(count) * rows, LANES), BF16),
+                    pltpu.VMEM((8 * per, LANES), F32),
+                    pltpu.SMEM((count + 1,), I32),
+                    pltpu.SMEM((count + 1,), I32),
+                    pltpu.SemaphoreType.DMA((count,)),
+                ]
+
+            kept = jax.ShapeDtypeStruct((heads // 2, rows, LANES), BF16)
+            out, acc = call(
+                functools.partial(attend_kernel, heads, blocks, 0, slides),
+                (kept, jax.ShapeDtypeStruct((heads, rows, LANES), F32)),
+                [SMEM, SMEM, VMEM] + [ANY] * 2,
+                (VMEM, VMEM),
+                scratch(2),
+                flops=10**9,
+                moved=8 * 10**6,
+            )(meta, slide_len, q, got[0], got[1])
             for m in range(1, nz):
                 got[2 * m + 1] = lax.ppermute(got[2 * m], "sub", swap)
-            refs = [got[m] for m in range(blocks)]
             out = call(
-                functools.partial(attend_kernel, heads, blocks, slides),
-                jax.ShapeDtypeStruct((heads // 2, rows, LANES), BF16),
-                [SMEM, SMEM, VMEM] + [ANY] * blocks,
+                functools.partial(attend_kernel, heads, blocks, 2, slides),
+                kept,
+                [SMEM, SMEM, VMEM, VMEM, VMEM] + [ANY] * (blocks - 2),
                 VMEM,
-                [
-                    pltpu.VMEM((blocks, full * per, LANES), BF16),
-                    pltpu.VMEM((blocks * rows, LANES), BF16),
-                    pltpu.VMEM((rows, LANES), F32),
-                    pltpu.SMEM((blocks + 1,), I32),
-                    pltpu.SMEM((blocks + 1,), I32),
-                    pltpu.SemaphoreType.DMA((blocks,)),
-                ],
-                vmem=6 + (blocks + 2) * full * per * LANES * 2 // MIB,
-            )(meta, slide_len, q, *refs)
+                scratch(blocks - 2),
+                vmem=10 + blocks * full * per * LANES * 2 // MIB + blocks * rows * LANES * 4 // MIB,
+            )(meta, slide_len, q, out, acc, *(got[m] for m in range(2, blocks)))
             return out, tok_sums, wide, rep_got
 
         return run
@@ -564,15 +641,25 @@
             step *= 2
         got = lax.ppermute(terms, "head", swap)
         other = lax.ppermute(sums, "head", swap)
+        unpermuted = pltpu.VMEM((cols // LANES, rows, LANES), F32)
+        y = call(
+            own_kernel,
+            jax.ShapeDtypeStruct((rows, cols), F32),
+            [VMEM] * 3,
+            VMEM,
+            [unpermuted],
+            flops=10**9,
+            moved=4 * 10**6,
+        )(tokens, out, wide)
         mixed = call(
             mix_kernel,
             jax.ShapeDtypeStruct((rows, cols), BF16),
-            [VMEM] * 4,
+            [VMEM] * 2,
             VMEM,
-            [pltpu.VMEM((cols // LANES, rows, LANES), F32)],
-            flops=10**9,
-            moved=4 * 10**6,
-        )(tokens, out, wide, got)
+            [unpermuted],
+            flops=10**8,
+            moved=2 * 10**6,
+        )(y, got)
         reps = (reports, rep_got)
     else:
         sums = lax.psum(sums, ("ctx", "sub", "head"))

time: 60.7 us -> 56.2 us (0.926)
  local copies, waits for them, and re-layouts: 2.77 us -> 0.13 us
  starting transfers between devices: 19 us -> 16.7 us
  Pallas kernels: 21.1 us -> 23.3 us
  waiting for transfers between devices: 15.5 us -> 13.7 us
    ppermute x2, starting transfers between devices: 7.52 us -> 3.99 us  [run_device(): sums = sums + lax.ppermute(sums, 'ctx', [(i, i ^ step) for i in range(nz)])]
    pallas_call x2 -> x4, Pallas kernels: 8.29 us -> 11 us  [the longest x1 5.94 us: run(): call(functools.partial(attend_kernel, heads, blocks, 0, slides), (kept, j...]
    unnamed x26 -> x12, local copies, waits for them, and re-layouts: 2.71 us -> 0.03 us
    ppermute x1, starting transfers between devices: 0.4 us -> 2.2 us  [run_device(): sums = sums + lax.ppermute(sums, 'sub', swap)]
    ppermute x3, waiting for transfers between devices: 9.64 us -> 7.84 us  [run(): got[2 * m] = lax.ppermute(pack[:mid if m == 1 else far], 'ctx', ends)]
    ppermute x1, waiting for transfers between devices: 1.24 us -> 0.01 us  [run_device(): other = lax.ppermute(sums, 'head', swap)]
    ppermute x2, waiting for transfers between devices: 3.79 us -> 4.98 us  [run_device(): sums = sums + lax.ppermute(sums, 'ctx', [(i, i ^ step) for i in range(nz)])]
    ppermute x3, starting transfers between devices: 6.58 us -> 5.96 us  [run(): got[2 * m] = lax.ppermute(pack[:mid if m == 1 else far], 'ctx', ends)]
  transfers between devices with their start and end apart: 13 -> 13, of which waited for: 6 -> 4; matrix products, arithmetic and copies ran while one was open for 0% -> 0% of each run, Pallas kernels for 21% -> 28%
where the time goes in v2:
time: 56.2 us; the launch traced here: 56 us
  Pallas kernels  23.3 us (41%)
  starting transfers between devices  16.7 us (30%)
  waiting for transfers between devices  13.7 us (24%)
  between operations  1.46 us (3%)
  loops' own time  0.65 us (1%)
    ppermute x3, waiting for transfers between devices, run(): got[2 * m] = lax.ppermute(pack[:mid if m == 1 else far], 'ctx', ends)  7.84 us
    ppermute x3, starting transfers between devices, run(): got[2 * m] = lax.ppermute(pack[:mid if m == 1 else far], 'ctx', ends)  5.96 us
    pallas_call x1, Pallas kernels, run(): call(functools.partial(attend_kernel, heads, blocks, 0, slides), (kept, j...  5.94 us
    pallas_call x1, Pallas kernels, run_device(): call(functools.partial(keys_kernel, ladder, heads, nx, classes, slides),...  5.05 us
    ppermute x2, waiting for transfers between devices, run_device(): sums = sums + lax.ppermute(sums, 'ctx', [(i, i ^ step) for i in range(nz)])  4.98 us
    ppermute x2, starting transfers between devices, run_device(): sums = sums + lax.ppermute(sums, 'ctx', [(i, i ^ step) for i in range(nz)])  3.99 us
    pallas_call x1, Pallas kernels, run(): call(functools.partial(queries_kernel, heads, slides, blocks), (jax.Shape...  3.93 us
    ppermute x1, starting transfers between devices, run_device(): sums = sums + lax.ppermute(sums, 'sub', swap)  2.2 us
  transfers between devices with their start and end apart: 13, of which 4 were waited for; matrix products, arithmetic and copies ran while one was open for 0% of the time, Pallas kernels for 28%

profile of v2, /device:TPU:0, one launch (start us, length us, event | category | flops | bytes accessed | tf_op | source)
XLA Modules:
  0.0 56.0 jit_solution(18399635418952710128)
XLA Ops:
  0.6 0.0 copy-start.1
  0.6 0.0 copy-start.2
  0.7 0.0 copy-start.18
  0.7 5.1 %shard_map.139 = (bf16[4096,128]{1,0:T(8,128)(2,1)S(1)}, bf16[512,768]{1,0:T(8,128)(2,1)S(1)}, s32[36]{0:T(128)S(1)}) custom-call(s32[16]{0:T(128)} %seg_hbm.1, s32[16]{0:T(128)} %dil_hbm.1, s32[8]{0:T(128)} %len_ref.3, bf16[512,768]{1,0:T(8,128)(2,1)} %x_ref.1, f32[768]{0:T(1024)} %ng_hbm.1, bf16[3,768,384]{2,1,0:T(8,128)(2,1)} %bitcast.3, f32[384]{0:T(512)} %kg_hbm.1), custom_call_target="tpu_custom_call" | custom-call | flops 1000000 | bytes 1000000 | tf_op jit(solution)/shard_map/pallas_call | solution.py:535
  5.8 0.0 copy-done.1
  5.8 0.0 copy-done.2
  5.8 0.0 copy-done.18
  5.8 0.0 copy-done.19
  5.8 29.0 %conditional.1 = (bf16[4,512,128]{2,1,0:T(8,128)(2,1)S(1)}, f32[8,1024]{1,0:T(8,128)S(1)}, bf16[512,768]{1,0:T(8,128)(2,1)S(1)}, bf16[256,384]{1,0:T(8,128)(2,1)}) conditional(s32[]{:T(128)} %bitcast.1, (s32[8]{0:T(128)S(1)}, bf16[512,768]{1,0:T(8,128)(2,1)S(1)}, bf16[512,768]{1,0:T(8,128)(2,1)S(1)}, ...), branch_computations={%region_0.0_spmd, %region_1.0_spmd, %region_2.0_spmd, %region_3.0_... | conditional | flops 2000999936 | bytes 43146912 | solution.py:622
  5.8 0.0 copy-start.11
  5.8 0.0 copy-start.3
  5.9 0.1 slice.27
  5.9 0.6 collective-permute-start
  6.5 2.6 %collective-permute-start.1 = (bf16[1216,128]{1,0:T(8,128)(2,1)S(1)}, bf16[1216,128]{1,0:T(8,128)(2,1)S(1)}, u32[]{:S(2)}, u32[]{:S(2)}) collective-permute-start(bf16[1216,128]{1,0:T(8,128)(2,1)S(1)} %slice.33), channel_id=1, source_target_pairs={{0,4},{4,0},{8,12},{12,8},{1,5},{5,1},{9,13},{13,9},{2,6},{6,2},{1... | collective-permute-start | bytes 933896 | tf_op jit(solution)/shard_map/cond/branch_0_fun/ppermute | solution.py:568
  9.2 2.7 %collective-permute-start.3 = (bf16[576,128]{1,0:T(8,128)(2,1)S(1)}, bf16[576,128]{1,0:T(8,128)(2,1)S(1)}, u32[]{:S(2)}, u32[]{:S(2)}) collective-permute-start(bf16[576,128]{1,0:T(8,128)(2,1)S(1)} %slice.44), channel_id=1, source_target_pairs={{0,8},{4,12},{8,0},{12,4},{1,9},{5,13},{9,1},{13,5},{2,10},{6,14},... | collective-permute-start | bytes 442376 | tf_op jit(solution)/shard_map/cond/branch_0_fun/ppermute | solution.py:568
  11.8 0.7 %collective-permute-start.5 = (bf16[576,128]{1,0:T(8,128)(2,1)S(1)}, bf16[576,128]{1,0:T(8,128)(2,1)S(1)}, u32[]{:S(2)}, u32[]{:S(2)}) collective-permute-start(bf16[576,128]{1,0:T(8,128)(2,1)S(1)} %slice.44), channel_id=1, source_target_pairs={{4,8},{8,4},{5,9},{9,5},{6,10},{10,6},{7,11},{11,7},{20,24},{24,20... | collective-permute-start | bytes 442376 | tf_op jit(solution)/shard_map/cond/branch_0_fun/ppermute | solution.py:568
  12.5 7.8 %collective-permute-done.1.rest_2_ = bf16[1216,128]{1,0:T(8,128)(2,1)S(1)} collective-permute-done((bf16[1216,128]{1,0:T(8,128)(2,1)S(1)}, bf16[1216,128]{1,0:T(8,128)(2,1)S(1)}, u32[]{:S(2)}, u32[]{:S(2)}) %collective-permute-start.1) | collective-permute-done | bytes 311328 | tf_op jit(solution)/shard_map/cond/branch_0_fun/ppermute | solution.py:568
  20.3 0.0 collective-permute-start.2
  20.3 1.6 %collective-permute-start.7 = (bf16[256,384]{1,0:T(8,128)(2,1)S(1)}, bf16[256,384]{1,0:T(8,128)(2,1)}, u32[]{:S(2)}, u32[]{:S(2)}) collective-permute-start(bf16[256,384]{1,0:T(8,128)(2,1)S(1)} %copy-done.11), channel_id=1, source_target_pairs={{0,2},{2,0},{1,3},{3,1},{4,6},{6,4},{5,7},{7,5},{8,10},{10,8},{9,1... | collective-permute-start | bytes 589832 | tf_op jit(solution)/shard_map/cond/branch_0_fun/ppermute | solution.py:571
  21.9 0.0 collective-permute-done.3.rest_4_
  21.9 0.2 collective-permute-start.4
  22.1 0.0 collective-permute-done.5.rest_6_
  22.1 0.3 collective-permute-start.6
  22.4 0.0 copy-done.3
  22.4 3.9 %branch_0_fun.3 = (bf16[8,512,128]{2,1,0:T(8,128)(2,1)S(1)}, f32[8,1024]{1,0:T(8,128)S(1)}, bf16[512,768]{1,0:T(8,128)(2,1)S(1)}) custom-call(s32[8]{0:T(128)S(1)} %get-tuple-element.145.len_ref, bf16[512,768]{1,0:T(8,128)(2,1)S(1)} %get-tuple-element.146.x_ref, bf16[512,768]{1,0:T(8,128)(2,1)S(1)} %get-tuple-element.147.normed_ref, ...), custom_call_target="tpu_custom_call" | custom-call | flops 1000000000 | bytes 4000000 | tf_op jit(solution)/shard_map/cond/branch_0_fun/pallas_call | solution.py:574
  26.3 0.0 collective-permute-done.rest_1_
  26.3 5.9 %branch_0_fun.4 = (bf16[4,512,128]{2,1,0:T(8,128)(2,1)S(1)}, f32[8,512,128]{2,1,0:T(8,128)S(1)}) custom-call(s32[36]{0:T(128)S(1)} %get-tuple-element.144.meta_ref, s32[8]{0:T(128)S(1)} %get-tuple-element.145.len_ref, bf16[8,512,128]{2,1,0:T(8,128)(2,1)S(1)} %get-tuple-element.152.q_ref, bf16[4096,128]{1,0:T(8,128)(2,1)S(1)} %get-tuple-element.153.rest_0_, ...), custom_call_target="tpu_custom_call" | custom-call | flops 1000000000 | bytes 8000000 | tf_op jit(solution)/shard_map/cond/branch_0_fun/pallas_call | solution.py:599
  32.3 0.0 collective-permute-done.4.rest_5_
  32.3 0.0 collective-permute-done.6.rest_7_
  32.3 0.0 collective-permute-done.2.rest_3_
  32.3 1.9 %branch_0_fun.5 = bf16[4,512,128]{2,1,0:T(8,128)(2,1)S(1)} custom-call(s32[36]{0:T(128)S(1)} %get-tuple-element.144.meta_ref, s32[8]{0:T(128)S(1)} %get-tuple-element.145.len_ref, bf16[8,512,128]{2,1,0:T(8,128)(2,1)S(1)} %get-tuple-element.152.q_ref, bf16[4,512,128]{2,1,0:T(8,128)(2,1)S(1)} %get-tuple-element.154.rest_0_, ...), custom_call_target="tpu_custom_call" | custom-call | flops 1000000 | bytes 1000000 | tf_op jit(solution)/shard_map/cond/branch_0_fun/pallas_call | solution.py:610
  34.2 0.0 collective-permute-done.7
  34.8 1.6 %shard_map.141 = (bf16[512,384]{1,0:T(8,128)(2,1)S(1)}, f32[8,1024]{1,0:T(8,128)S(1)}) custom-call(s32[8]{0:T(128)S(1)} %copy-done.18, f32[8,1024]{1,0:T(8,128)S(1)} %get-tuple-element.275.tok_sums_ref, bf16[4,512,128]{2,1,0:T(8,128)(2,1)S(1)} %get-tuple-element.273.out_ref, bf16[512,768]{1,0:T(8,128)(2,1)S(1)} %get-tuple-element.274.wide_ref), custom_call_target="tpu_custom_call" | custom-call | flops 1000000 | bytes 1000000 | tf_op jit(solution)/shard_map/pallas_call | solution.py:627
  36.4 0.0 copy-start
  36.4 0.0 copy-start.10
  36.4 0.1 collective-permute-start.64
  36.5 2.2 %collective-permute-start.65 = (f32[8,1024]{1,0:T(8,128)S(1)}, f32[8,1024]{1,0:T(8,128)S(1)}, u32[]{:S(2)}, u32[]{:S(2)}) collective-permute-start(f32[8,1024]{1,0:T(8,128)S(1)} %get-tuple-element.277), channel_id=1, source_target_pairs={{0,1},{1,0},{2,3},{3,2},{4,5},{5,4},{6,7},{7,6},{8,9},{9,8},{10,11... | collective-permute-start | bytes 98312 | tf_op jit(solution)/shard_map/ppermute | solution.py:637
  38.7 0.9 %collective-permute-done.65 = f32[8,1024]{1,0:T(8,128)S(1)} collective-permute-done((f32[8,1024]{1,0:T(8,128)S(1)}, f32[8,1024]{1,0:T(8,128)S(1)}, u32[]{:S(2)}, u32[]{:S(2)}) %collective-permute-start.65) | collective-permute-done | bytes 32800 | tf_op jit(solution)/shard_map/ppermute | solution.py:637
  39.5 1.3 %collective-permute-start.66 = (f32[8,1024]{1,0:T(8,128)S(1)}, f32[8,1024]{1,0:T(8,128)S(1)}, u32[]{:S(2)}, u32[]{:S(2)}) collective-permute-start(f32[8,1024]{1,0:T(8,128)S(1)} %add.9), channel_id=1, source_target_pairs={{0,4},{4,0},{8,12},{12,8},{1,5},{5,1},{9,13},{13,9},{2,6},{6,2},{1... | collective-permute-start | bytes 98312 | tf_op jit(solution)/shard_map/ppermute | solution.py:640
  40.9 2.6 %collective-permute-done.66 = f32[8,1024]{1,0:T(8,128)S(1)} collective-permute-done((f32[8,1024]{1,0:T(8,128)S(1)}, f32[8,1024]{1,0:T(8,128)S(1)}, u32[]{:S(2)}, u32[]{:S(2)}) %collective-permute-start.66) | collective-permute-done | bytes 32800 | tf_op jit(solution)/shard_map/ppermute | solution.py:640
  43.5 2.7 %collective-permute-start.67 = (f32[8,1024]{1,0:T(8,128)S(1)}, f32[8,1024]{1,0:T(8,128)S(1)}, u32[]{:S(2)}, u32[]{:S(2)}) collective-permute-start(f32[8,1024]{1,0:T(8,128)S(1)} %add.10), channel_id=1, source_target_pairs={{0,8},{4,12},{8,0},{12,4},{1,9},{5,13},{9,1},{13,5},{2,10},{6,14},... | collective-permute-start | bytes 98312 | tf_op jit(solution)/shard_map/ppermute | solution.py:640
  46.1 2.4 %collective-permute-done.67 = f32[8,1024]{1,0:T(8,128)S(1)} collective-permute-done((f32[8,1024]{1,0:T(8,128)S(1)}, f32[8,1024]{1,0:T(8,128)S(1)}, u32[]{:S(2)}, u32[]{:S(2)}) %collective-permute-start.67) | collective-permute-done | bytes 32800 | tf_op jit(solution)/shard_map/ppermute | solution.py:640
  48.5 1.8 %collective-permute-start.68 = (f32[8,1024]{1,0:T(8,128)S(1)}, f32[8,1024]{1,0:T(8,128)S(1)}, u32[]{:S(2)}, u32[]{:S(2)}) collective-permute-start(f32[8,1024]{1,0:T(8,128)S(1)} %add.11.sums_ref), channel_id=1, source_target_pairs={{0,2},{2,0},{1,3},{3,1},{4,6},{6,4},{5,7},{7,5},{8,10},{10,8},{9,1... | collective-permute-start | bytes 98312 | tf_op jit(solution)/shard_map/ppermute | solution.py:643
  50.3 1.9 %shard_map.140.y_ref = f32[512,384]{1,0:T(8,128)S(1)} custom-call(bf16[512,768]{1,0:T(8,128)(2,1)} %x_ref.1, bf16[4,512,128]{2,1,0:T(8,128)(2,1)S(1)} %get-tuple-element.273.out_ref, bf16[512,768]{1,0:T(8,128)(2,1)S(1)} %get-tuple-element.274.wide_ref), custom_call_target="tpu_custom_call" | custom-call | flops 1000000000 | bytes 4000000 | tf_op jit(solution)/shard_map/pallas_call | solution.py:645
  52.9 0.0 collective-permute-done.68.other_ref
  52.9 1.8 %shard_map.143 = (f32[8,256]{1,0:T(8,128)}, f32[8]{0:T(128)}) custom-call(s32[8]{0:T(128)S(1)} %copy-done.18, s32[8]{0:T(128)S(1)} %copy-done, f32[1]{0:T(128)S(6)} %copy.47.scale_ref, f32[8,1024]{1,0:T(8,128)S(1)} %add.11.sums_ref, f32[8,1024]{1,0:T(8,128)S(1)} %collective-permute-done.68.other_ref, bf16[256,384]{1,0:T(8,128)(2,1)S(1)} %copy-done.10, ...), custom_call_target="tpu_custom_call" | custom-call | flops 1000000 | bytes 1000000 | tf_op jit(solution)/shard_map/pallas_call | solution.py:673
  54.7 0.0 collective-permute-done.64.got_ref
  54.7 1.2 %shard_map.142 = bf16[512,384]{1,0:T(8,128)(2,1)} custom-call(f32[512,384]{1,0:T(8,128)S(1)} %shard_map.140.y_ref, bf16[512,384]{1,0:T(8,128)(2,1)S(1)} %collective-permute-done.64.got_ref), custom_call_target="tpu_custom_call" | custom-call | flops 100000000 | bytes 2000000 | tf_op jit(solution)/shard_map/pallas_call | solution.py:654
  (9 shorter events, 0.1 us)
Async XLA Ops:
  0.6 5.1 %copy-start.1 = (bf16[768,3,384]{2,0,1:T(8,128)(2,1)S(1)}, bf16[768,3,384]{2,0,1:T(8,128)(2,1)}, u32[]{:S(2)}) copy-start(bf16[768,3,384]{2,0,1:T(8,128)(2,1)} %param.22) | copy-start | bytes 5308420
  0.6 5.1 %copy-start.2 = (bf16[512,768]{1,0:T(8,128)(2,1)S(1)}, bf16[512,768]{1,0:T(8,128)(2,1)}, u32[]{:S(2)}) copy-start(bf16[512,768]{1,0:T(8,128)(2,1)} %x_ref.1) | copy-start | bytes 2359300
  0.7 5.1 %copy-start.18 = (s32[8]{0:T(128)S(1)}, s32[8]{0:T(128)}, u32[]{:S(2)}) copy-start(s32[8]{0:T(128)} %len_ref.3) | copy-start | bytes 100
  0.7 5.1 %copy-start.19 = (f32[384]{0:T(512)S(1)}, f32[384]{0:T(512)}, u32[]{:S(2)}) copy-start(f32[384]{0:T(512)} %param.23) | copy-start | bytes 4612
  5.8 14.5 %copy-start.11 = (bf16[256,384]{1,0:T(8,128)(2,1)S(1)}, bf16[256,384]{1,0:T(8,128)(2,1)}, u32[]{:S(2)}) copy-start(bf16[256,384]{1,0:T(8,128)(2,1)} %get-tuple-element.151.rep_ref) | copy-start | bytes 589828 | tf_op jit(solution)/shard_map/cond
  5.8 16.6 %copy-start.3 = (bf16[384,768]{1,0:T(8,128)(2,1)S(1)}, bf16[384,768]{1,0:T(8,128)(2,1)}, u32[]{:S(2)}) copy-start(bf16[384,768]{1,0:T(8,128)(2,1)} %get-tuple-element.150.w_out_ref) | copy-start | bytes 1769476 | tf_op jit(solution)/shard_map/cond
  5.9 20.4 %collective-permute-start = (bf16[3072,128]{1,0:T(8,128)(2,1)S(1)}, bf16[3072,128]{1,0:T(8,128)(2,1)S(1)}, u32[]{:S(2)}, u32[]{:S(2)}) collective-permute-start(bf16[3072,128]{1,0:T(8,128)(2,1)S(1)} %slice.27), channel_id=1, source_target_pairs={{0,1},{1,0},{2,3},{3,2},{4,5},{5,4},{6,7},{7,6},{8,9},{9,8},{10,11... | collective-permute-start | bytes 2359304 | tf_op jit(solution)/shard_map/cond/branch_0_fun/ppermute | solution.py:569
  6.5 13.8 %collective-permute-start.1 = (bf16[1216,128]{1,0:T(8,128)(2,1)S(1)}, bf16[1216,128]{1,0:T(8,128)(2,1)S(1)}, u32[]{:S(2)}, u32[]{:S(2)}) collective-permute-start(bf16[1216,128]{1,0:T(8,128)(2,1)S(1)} %slice.33), channel_id=1, source_target_pairs={{0,4},{4,0},{8,12},{12,8},{1,5},{5,1},{9,13},{13,9},{2,6},{6,2},{1... | collective-permute-start | bytes 933896 | tf_op jit(solution)/shard_map/cond/branch_0_fun/ppermute | solution.py:568
  9.2 12.7 %collective-permute-start.3 = (bf16[576,128]{1,0:T(8,128)(2,1)S(1)}, bf16[576,128]{1,0:T(8,128)(2,1)S(1)}, u32[]{:S(2)}, u32[]{:S(2)}) collective-permute-start(bf16[576,128]{1,0:T(8,128)(2,1)S(1)} %slice.44), channel_id=1, source_target_pairs={{0,8},{4,12},{8,0},{12,4},{1,9},{5,13},{9,1},{13,5},{2,10},{6,14},... | collective-permute-start | bytes 442376 | tf_op jit(solution)/shard_map/cond/branch_0_fun/ppermute | solution.py:568
  11.8 10.3 %collective-permute-start.5 = (bf16[576,128]{1,0:T(8,128)(2,1)S(1)}, bf16[576,128]{1,0:T(8,128)(2,1)S(1)}, u32[]{:S(2)}, u32[]{:S(2)}) collective-permute-start(bf16[576,128]{1,0:T(8,128)(2,1)S(1)} %slice.44), channel_id=1, source_target_pairs={{4,8},{8,4},{5,9},{9,5},{6,10},{10,6},{7,11},{11,7},{20,24},{24,20... | collective-permute-start | bytes 442376 | tf_op jit(solution)/shard_map/cond/branch_0_fun/ppermute | solution.py:568
  20.3 12.0 %collective-permute-start.2 = (bf16[1216,128]{1,0:T(8,128)(2,1)S(1)}, bf16[1216,128]{1,0:T(8,128)(2,1)S(1)}, u32[]{:S(2)}, u32[]{:S(2)}) collective-permute-start(bf16[1216,128]{1,0:T(8,128)(2,1)S(1)} %collective-permute-done.1.rest_2_), channel_id=1, source_target_pairs={{0,1},{1,0},{2,3},{3,2},{4,5},{5,4},{6,7},{7,6},{8,9},{9,8},{10,11... | collective-permute-start | bytes 933896 | tf_op jit(solution)/shard_map/cond/branch_0_fun/ppermute | solution.py:609
  20.3 13.9 %collective-permute-start.7 = (bf16[256,384]{1,0:T(8,128)(2,1)S(1)}, bf16[256,384]{1,0:T(8,128)(2,1)}, u32[]{:S(2)}, u32[]{:S(2)}) collective-permute-start(bf16[256,384]{1,0:T(8,128)(2,1)S(1)} %copy-done.11), channel_id=1, source_target_pairs={{0,2},{2,0},{1,3},{3,1},{4,6},{6,4},{5,7},{7,5},{8,10},{10,8},{9,1... | collective-permute-start | bytes 589832 | tf_op jit(solution)/shard_map/cond/branch_0_fun/ppermute | solution.py:571
  21.9 10.4 %collective-permute-start.4 = (bf16[576,128]{1,0:T(8,128)(2,1)S(1)}, bf16[576,128]{1,0:T(8,128)(2,1)S(1)}, u32[]{:S(2)}, u32[]{:S(2)}) collective-permute-start(bf16[576,128]{1,0:T(8,128)(2,1)S(1)} %collective-permute-done.3.rest_4_), channel_id=1, source_target_pairs={{0,1},{1,0},{2,3},{3,2},{4,5},{5,4},{6,7},{7,6},{8,9},{9,8},{10,11... | collective-permute-start | bytes 442376 | tf_op jit(solution)/shard_map/cond/branch_0_fun/ppermute | solution.py:609
  22.1 10.2 %collective-permute-start.6 = (bf16[576,128]{1,0:T(8,128)(2,1)S(1)}, bf16[576,128]{1,0:T(8,128)(2,1)S(1)}, u32[]{:S(2)}, u32[]{:S(2)}) collective-permute-start(bf16[576,128]{1,0:T(8,128)(2,1)S(1)} %collective-permute-done.5.rest_6_), channel_id=1, source_target_pairs={{0,1},{1,0},{2,3},{3,2},{4,5},{5,4},{6,7},{7,6},{8,9},{9,8},{10,11... | collective-permute-start | bytes 442376 | tf_op jit(solution)/shard_map/cond/branch_0_fun/ppermute | solution.py:609
  36.4 16.5 %copy-start = (s32[8]{0:T(128)S(1)}, s32[8]{0:T(128)}, u32[]{:S(2)}) copy-start(s32[8]{0:T(128)} %pairs_ref.1) | copy-start | bytes 100
  36.4 16.5 %copy-start.10 = (bf16[256,384]{1,0:T(8,128)(2,1)S(1)}, bf16[256,384]{1,0:T(8,128)(2,1)}, u32[]{:S(2)}) copy-start(bf16[256,384]{1,0:T(8,128)(2,1)} %rest_0_.1) | copy-start | bytes 589828
  36.4 18.3 %collective-permute-start.64 = (bf16[512,384]{1,0:T(8,128)(2,1)S(1)}, bf16[512,384]{1,0:T(8,128)(2,1)S(1)}, u32[]{:S(2)}, u32[]{:S(2)}) collective-permute-start(bf16[512,384]{1,0:T(8,128)(2,1)S(1)} %get-tuple-element.276), channel_id=1, source_target_pairs={{0,2},{2,0},{1,3},{3,1},{4,6},{6,4},{5,7},{7,5},{8,10},{10,8},{9,1... | collective-permute-start | bytes 1179656 | tf_op jit(solution)/shard_map/ppermute | solution.py:642
  36.5 3.1 %collective-permute-start.65 = (f32[8,1024]{1,0:T(8,128)S(1)}, f32[8,1024]{1,0:T(8,128)S(1)}, u32[]{:S(2)}, u32[]{:S(2)}) collective-permute-start(f32[8,1024]{1,0:T(8,128)S(1)} %get-tuple-element.277), channel_id=1, source_target_pairs={{0,1},{1,0},{2,3},{3,2},{4,5},{5,4},{6,7},{7,6},{8,9},{9,8},{10,11... | collective-permute-start | bytes 98312 | tf_op jit(solution)/shard_map/ppermute | solution.py:637
  39.5 3.9 %collective-permute-start.66 = (f32[8,1024]{1,0:T(8,128)S(1)}, f32[8,1024]{1,0:T(8,128)S(1)}, u32[]{:S(2)}, u32[]{:S(2)}) collective-permute-start(f32[8,1024]{1,0:T(8,128)S(1)} %add.9), channel_id=1, source_target_pairs={{0,4},{4,0},{8,12},{12,8},{1,5},{5,1},{9,13},{13,9},{2,6},{6,2},{1... | collective-permute-start | bytes 98312 | tf_op jit(solution)/shard_map/ppermute | solution.py:640
  43.5 5.1 %collective-permute-start.67 = (f32[8,1024]{1,0:T(8,128)S(1)}, f32[8,1024]{1,0:T(8,128)S(1)}, u32[]{:S(2)}, u32[]{:S(2)}) collective-permute-start(f32[8,1024]{1,0:T(8,128)S(1)} %add.10), channel_id=1, source_target_pairs={{0,8},{4,12},{8,0},{12,4},{1,9},{5,13},{9,1},{13,5},{2,10},{6,14},... | collective-permute-start | bytes 98312 | tf_op jit(solution)/shard_map/ppermute | solution.py:640
  48.5 4.4 %collective-permute-start.68 = (f32[8,1024]{1,0:T(8,128)S(1)}, f32[8,1024]{1,0:T(8,128)S(1)}, u32[]{:S(2)}, u32[]{:S(2)}) collective-permute-start(f32[8,1024]{1,0:T(8,128)S(1)} %add.11.sums_ref), channel_id=1, source_target_pairs={{0,2},{2,0},{1,3},{3,1},{4,6},{6,4},{5,7},{7,5},{8,10},{10,8},{9,1... | collective-permute-start | bytes 98312 | tf_op jit(solution)/shard_map/ppermute | solution.py:643

commit v3 on v2

--- a/solution.py
+++ b/solution.py
@@ -287,15 +287,10 @@
         out_ref, *rest = rest
     else:
         out_ref, acc_out_ref, *rest = rest
-    kvs_ref, keys_ref, acc_ref, list_ref, before_ref, sem = rest
+    keys_ref, acc_ref, before_ref = rest
     rows = q_ref.shape[1]
     per = rows // RES
     me = lax.axis_index(("ctx", "sub"))
-    copies = []
-    for i, kv_ref in enumerate(kv_refs):
-        size = kv_ref.shape[0]
-        copies.append(pltpu.make_async_copy(kv_ref, kvs_ref.at[i, pl.ds(0, size), :], sem.at[i]))
-        copies[-1].start()
     low = jnp.int32(0)
     high = jnp.int32(rows * blocks)
     end = jnp.int32(0)
@@ -307,7 +302,6 @@
     for i, m in enumerate(range(begin, stop)):
         other = jnp.bitwise_xor(me, m) * rows
         before_ref[i] = count
-        list_ref[count] = jnp.int32(i)
         count = count + ((other < high) & (other + rows > low)).astype(I32)
     before_ref[stop - begin] = count
     out_ref[...] = jnp.zeros_like(out_ref) if begin == 0 else out_in_ref[...]
@@ -316,8 +310,6 @@
     for side in range(2):
         outside = outside | ((lane >= S_AT[side]) & (lane < S_AT[side] + slides))
     nothing = jnp.where(outside, -FAR, 0.0)
-    for copy in copies:
-        copy.wait()
     factor = math.log2(math.e) / math.sqrt(HEAD_DIM)
 
     def head_step(h, carry):
@@ -337,13 +329,19 @@
             tiles = (parts + (group - 1)) >> (group.bit_length() - 1)
             ours = (lane >= HALF) == (side == 1)
 
-            def take(i, carry):
-                block = lax.shift_right_logical(i, steps - 1)
-                at = off + (i & (steps - 1)) * size
-                keys_ref[pl.ds(pl.multiple_of(i * size, size), size), :] = kvs_ref[
-                    list_ref[block], pl.ds(pl.multiple_of(at, per), size), :
-                ]
-                return carry
+            for i, kv_ref in enumerate(kv_refs):
+                at = before_ref[i]
+
+                @pl.when((before_ref[i + 1] > at) & (at < some))
+                def _(kv_ref=kv_ref, at=at):
+                    def take(c, carry):
+                        to = (at * steps + c) * size
+                        keys_ref[pl.ds(pl.multiple_of(to, size), size), :] = kv_ref[
+                            pl.ds(pl.multiple_of(off + c * size, per), size), :
+                        ]
+                        return carry
+
+                    lax.fori_loop(0, steps, take, 0)
 
             def fill(i, carry):
                 keys_ref[pl.ds(pl.multiple_of(i * size, size), size), :] = jnp.broadcast_to(
@@ -351,7 +349,6 @@
                 ).astype(BF16)
                 return carry
 
-            lax.fori_loop(0, parts, take, 0)
             lax.fori_loop(parts, tiles * group, fill, 0)
 
             def q_step(i, carry):
@@ -587,19 +584,16 @@
 
             def scratch(count):
                 return [
-                    pltpu.VMEM((count, full * per, LANES), BF16),
                     pltpu.VMEM((pl.next_power_of_2(count) * rows, LANES), BF16),
                     pltpu.VMEM((8 * per, LANES), F32),
                     pltpu.SMEM((count + 1,), I32),
-                    pltpu.SMEM((count + 1,), I32),
-                    pltpu.SemaphoreType.DMA((count,)),
                 ]
 
             kept = jax.ShapeDtypeStruct((heads // 2, rows, LANES), BF16)
             out, acc = call(
                 functools.partial(attend_kernel, heads, blocks, 0, slides),
                 (kept, jax.ShapeDtypeStruct((heads, rows, LANES), F32)),
-                [SMEM, SMEM, VMEM] + [ANY] * 2,
+                [SMEM, SMEM, VMEM] + [VMEM] * 2,
                 (VMEM, VMEM),
                 scratch(2),
                 flops=10**9,
@@ -610,7 +604,7 @@
             out = call(
                 functools.partial(attend_kernel, heads, blocks, 2, slides),
                 kept,
-                [SMEM, SMEM, VMEM, VMEM, VMEM] + [ANY] * (blocks - 2),
+                [SMEM, SMEM, VMEM, VMEM, VMEM] + [VMEM] * (blocks - 2),
                 VMEM,
                 scratch(blocks - 2),
                 vmem=10 + blocks * full * per * LANES * 2 // MIB + blocks * rows * LANES * 4 // MIB,
@@ -634,13 +628,14 @@
         (VMEM, VMEM),
     )(slide_len, tok_sums, out, wide)
     if nx == 2:
-        sums = sums + lax.ppermute(sums, "sub", swap)
+        sums = sums + lax.ppermute(sums, "head", swap)
+        got = lax.ppermute(terms, "head", swap)
+        other = lax.ppermute(sums, "sub", swap)
         step = 1
         while step < nz:
-            sums = sums + lax.ppermute(sums, "ctx", [(i, i ^ step) for i in range(nz)])
+            sums = sums + other
+            other = lax.ppermute(sums, "ctx", [(i, i ^ step) for i in range(nz)])
             step *= 2
-        got = lax.ppermute(terms, "head", swap)
-        other = lax.ppermute(sums, "head", swap)
         unpermuted = pltpu.VMEM((cols // LANES, rows, LANES), F32)
         y = call(
             own_kernel,

time: 56.2 us -> 62.9 us (1.12)
  waiting for transfers between devices: 13.7 us -> 19.9 us
  starting transfers between devices: 16.7 us -> 18.2 us
  Pallas kernels: 23.3 us -> 22.2 us
    ppermute x4, waiting for transfers between devices: 5.84 us -> 12.1 us  [the longest x1 9.32 us: run_device(): sums = sums + lax.ppermute(sums, 'head', swap)]
    ppermute x4, starting transfers between devices: 8 us -> 9.59 us  [the longest x2 6.4 us: run_device(): other = lax.ppermute(sums, 'ctx', [(i, i ^ step) for i in range(nz)])]
    pallas_call x1, Pallas kernels: 1.91 us -> 0.92 us  [run(): call(functools.partial(attend_kernel, heads, blocks, 2, slides), kept, [S...]
  transfers between devices with their start and end apart: 13 -> 13, of which waited for: 4 -> 4; matrix products, arithmetic and copies ran while one was open for 0% -> 0% of each run, Pallas kernels for 28% -> 23%
where the time goes in v3:
time: 62.9 us; the launch traced here: 62.7 us
  Pallas kernels  22.2 us (35%)
  waiting for transfers between devices  19.9 us (32%)
  starting transfers between devices  18.2 us (29%)
  between operations  1.46 us (2%)
  loops' own time  0.65 us (1%)
    ppermute x1, waiting for transfers between devices, run_device(): sums = sums + lax.ppermute(sums, 'head', swap)  9.32 us
    ppermute x3, waiting for transfers between devices, run(): got[2 * m] = lax.ppermute(pack[:mid if m == 1 else far], 'ctx', ends)  7.84 us
    ppermute x2, starting transfers between devices, run_device(): other = lax.ppermute(sums, 'ctx', [(i, i ^ step) for i in range(nz)])  6.4 us
    ppermute x3, starting transfers between devices, run(): got[2 * m] = lax.ppermute(pack[:mid if m == 1 else far], 'ctx', ends)  5.96 us
    pallas_call x1, Pallas kernels, run(): call(functools.partial(attend_kernel, heads, blocks, 0, slides), (kept, j...  5.81 us
    pallas_call x1, Pallas kernels, run_device(): call(functools.partial(keys_kernel, ladder, heads, nx, classes, slides),...  5.05 us
    pallas_call x1, Pallas kernels, run(): call(functools.partial(queries_kernel, heads, slides, blocks), (jax.Shape...  3.93 us
    ppermute x1, starting transfers between devices, run_device(): sums = sums + lax.ppermute(sums, 'head', swap)  2.01 us
  transfers between devices with their start and end apart: 13, of which 4 were waited for; matrix products, arithmetic and copies ran while one was open for 0% of the time, Pallas kernels for 23%

profile of v3, /device:TPU:0, one launch (start us, length us, event | category | flops | bytes accessed | tf_op | source)
XLA Modules:
  0.0 62.7 jit_solution(15006563435804382135)
XLA Ops:
  0.6 0.0 copy-start.1
  0.6 0.0 copy-start.2
  0.7 0.0 copy-start.18
  0.7 5.1 %shard_map.139 = (bf16[4096,128]{1,0:T(8,128)(2,1)S(1)}, bf16[512,768]{1,0:T(8,128)(2,1)S(1)}, s32[36]{0:T(128)S(1)}) custom-call(s32[16]{0:T(128)} %seg_hbm.1, s32[16]{0:T(128)} %dil_hbm.1, s32[8]{0:T(128)} %len_ref.3, bf16[512,768]{1,0:T(8,128)(2,1)} %x_ref.1, f32[768]{0:T(1024)} %ng_hbm.1, bf16[3,768,384]{2,1,0:T(8,128)(2,1)} %bitcast.3, f32[384]{0:T(512)} %kg_hbm.1), custom_call_target="tpu_custom_call" | custom-call | flops 1000000 | bytes 1000000 | tf_op jit(solution)/shard_map/pallas_call | solution.py:532
  5.8 0.0 copy-done.1
  5.8 0.0 copy-done.2
  5.8 0.0 copy-done.18
  5.8 0.0 copy-done.19
  5.8 27.8 %conditional.1 = (bf16[4,512,128]{2,1,0:T(8,128)(2,1)S(1)}, f32[8,1024]{1,0:T(8,128)S(1)}, bf16[512,768]{1,0:T(8,128)(2,1)S(1)}, bf16[256,384]{1,0:T(8,128)(2,1)}) conditional(s32[]{:T(128)} %bitcast.1, (s32[8]{0:T(128)S(1)}, bf16[512,768]{1,0:T(8,128)(2,1)S(1)}, bf16[512,768]{1,0:T(8,128)(2,1)S(1)}, ...), branch_computations={%region_0.0_spmd, %region_1.0_spmd, %region_2.0_spmd, %region_3.0_... | conditional | flops 2000999936 | bytes 43146912 | solution.py:616
  5.8 0.0 copy-start.11
  5.8 0.0 copy-start.3
  5.9 0.1 slice.27
  5.9 0.6 collective-permute-start
  6.5 2.6 %collective-permute-start.1 = (bf16[1216,128]{1,0:T(8,128)(2,1)S(1)}, bf16[1216,128]{1,0:T(8,128)(2,1)S(1)}, u32[]{:S(2)}, u32[]{:S(2)}) collective-permute-start(bf16[1216,128]{1,0:T(8,128)(2,1)S(1)} %slice.33), channel_id=1, source_target_pairs={{0,4},{4,0},{8,12},{12,8},{1,5},{5,1},{9,13},{13,9},{2,6},{6,2},{1... | collective-permute-start | bytes 933896 | tf_op jit(solution)/shard_map/cond/branch_0_fun/ppermute | solution.py:565
  9.2 2.7 %collective-permute-start.3 = (bf16[576,128]{1,0:T(8,128)(2,1)S(1)}, bf16[576,128]{1,0:T(8,128)(2,1)S(1)}, u32[]{:S(2)}, u32[]{:S(2)}) collective-permute-start(bf16[576,128]{1,0:T(8,128)(2,1)S(1)} %slice.44), channel_id=1, source_target_pairs={{0,8},{4,12},{8,0},{12,4},{1,9},{5,13},{9,1},{13,5},{2,10},{6,14},... | collective-permute-start | bytes 442376 | tf_op jit(solution)/shard_map/cond/branch_0_fun/ppermute | solution.py:565
  11.8 0.7 %collective-permute-start.5 = (bf16[576,128]{1,0:T(8,128)(2,1)S(1)}, bf16[576,128]{1,0:T(8,128)(2,1)S(1)}, u32[]{:S(2)}, u32[]{:S(2)}) collective-permute-start(bf16[576,128]{1,0:T(8,128)(2,1)S(1)} %slice.44), channel_id=1, source_target_pairs={{4,8},{8,4},{5,9},{9,5},{6,10},{10,6},{7,11},{11,7},{20,24},{24,20... | collective-permute-start | bytes 442376 | tf_op jit(solution)/shard_map/cond/branch_0_fun/ppermute | solution.py:565
  12.5 7.8 %collective-permute-done.1.rest_2_ = bf16[1216,128]{1,0:T(8,128)(2,1)S(1)} collective-permute-done((bf16[1216,128]{1,0:T(8,128)(2,1)S(1)}, bf16[1216,128]{1,0:T(8,128)(2,1)S(1)}, u32[]{:S(2)}, u32[]{:S(2)}) %collective-permute-start.1) | collective-permute-done | bytes 311328 | tf_op jit(solution)/shard_map/cond/branch_0_fun/ppermute | solution.py:565
  20.3 0.0 collective-permute-start.2
  20.3 1.6 %collective-permute-start.7 = (bf16[256,384]{1,0:T(8,128)(2,1)S(1)}, bf16[256,384]{1,0:T(8,128)(2,1)}, u32[]{:S(2)}, u32[]{:S(2)}) collective-permute-start(bf16[256,384]{1,0:T(8,128)(2,1)S(1)} %copy-done.11), channel_id=1, source_target_pairs={{0,2},{2,0},{1,3},{3,1},{4,6},{6,4},{5,7},{7,5},{8,10},{10,8},{9,1... | collective-permute-start | bytes 589832 | tf_op jit(solution)/shard_map/cond/branch_0_fun/ppermute | solution.py:568
  21.9 0.0 collective-permute-done.3.rest_4_
  21.9 0.2 collective-permute-start.4
  22.1 0.0 collective-permute-done.5.rest_6_
  22.1 0.3 collective-permute-start.6
  22.4 0.0 copy-done.3
  22.4 3.9 %branch_0_fun.3 = (bf16[8,512,128]{2,1,0:T(8,128)(2,1)S(1)}, f32[8,1024]{1,0:T(8,128)S(1)}, bf16[512,768]{1,0:T(8,128)(2,1)S(1)}) custom-call(s32[8]{0:T(128)S(1)} %get-tuple-element.145.len_ref, bf16[512,768]{1,0:T(8,128)(2,1)S(1)} %get-tuple-element.146.x_ref, bf16[512,768]{1,0:T(8,128)(2,1)S(1)} %get-tuple-element.147.normed_ref, ...), custom_call_target="tpu_custom_call" | custom-call | flops 1000000000 | bytes 4000000 | tf_op jit(solution)/shard_map/cond/branch_0_fun/pallas_call | solution.py:571
  26.3 0.0 collective-permute-done.rest_1_
  26.3 5.8 %branch_0_fun.4 = (bf16[4,512,128]{2,1,0:T(8,128)(2,1)S(1)}, f32[8,512,128]{2,1,0:T(8,128)S(1)}) custom-call(s32[36]{0:T(128)S(1)} %get-tuple-element.144.meta_ref, s32[8]{0:T(128)S(1)} %get-tuple-element.145.len_ref, bf16[8,512,128]{2,1,0:T(8,128)(2,1)S(1)} %get-tuple-element.152.q_ref, bf16[4096,128]{1,0:T(8,128)(2,1)S(1)} %get-tuple-element.153.rest_0_, ...), custom_call_target="tpu_custom_call" | custom-call | flops 1000000000 | bytes 8000000 | tf_op jit(solution)/shard_map/cond/branch_0_fun/pallas_call | solution.py:593
  32.1 0.0 collective-permute-done.4.rest_5_
  32.2 0.0 collective-permute-done.6.rest_7_
  32.2 0.0 collective-permute-done.2.rest_3_
  32.2 0.9 %branch_0_fun.5 = bf16[4,512,128]{2,1,0:T(8,128)(2,1)S(1)} custom-call(s32[36]{0:T(128)S(1)} %get-tuple-element.144.meta_ref, s32[8]{0:T(128)S(1)} %get-tuple-element.145.len_ref, bf16[8,512,128]{2,1,0:T(8,128)(2,1)S(1)} %get-tuple-element.152.q_ref, bf16[4,512,128]{2,1,0:T(8,128)(2,1)S(1)} %get-tuple-element.154.rest_0_, ...), custom_call_target="tpu_custom_call" | custom-call | flops 1000000 | bytes 1000000 | tf_op jit(solution)/shard_map/cond/branch_0_fun/pallas_call | solution.py:604
  33.1 0.0 collective-permute-done.7
  33.7 1.6 %shard_map.141 = (bf16[512,384]{1,0:T(8,128)(2,1)S(1)}, f32[8,1024]{1,0:T(8,128)S(1)}) custom-call(s32[8]{0:T(128)S(1)} %copy-done.18, f32[8,1024]{1,0:T(8,128)S(1)} %get-tuple-element.275.tok_sums_ref, bf16[4,512,128]{2,1,0:T(8,128)(2,1)S(1)} %get-tuple-element.273.out_ref, bf16[512,768]{1,0:T(8,128)(2,1)S(1)} %get-tuple-element.274.wide_ref), custom_call_target="tpu_custom_call" | custom-call | flops 1000000 | bytes 1000000 | tf_op jit(solution)/shard_map/pallas_call | solution.py:621
  35.3 0.0 copy-start
  35.3 0.0 copy-start.10
  35.3 0.1 collective-permute-start.64
  35.4 2.0 %collective-permute-start.65 = (f32[8,1024]{1,0:T(8,128)S(1)}, f32[8,1024]{1,0:T(8,128)S(1)}, u32[]{:S(2)}, u32[]{:S(2)}) collective-permute-start(f32[8,1024]{1,0:T(8,128)S(1)} %get-tuple-element.277), channel_id=1, source_target_pairs={{0,2},{2,0},{1,3},{3,1},{4,6},{6,4},{5,7},{7,5},{8,10},{10,8},{9,1... | collective-permute-start | bytes 98312 | tf_op jit(solution)/shard_map/ppermute | solution.py:631
  37.4 9.3 %collective-permute-done.65 = f32[8,1024]{1,0:T(8,128)S(1)} collective-permute-done((f32[8,1024]{1,0:T(8,128)S(1)}, f32[8,1024]{1,0:T(8,128)S(1)}, u32[]{:S(2)}, u32[]{:S(2)}) %collective-permute-start.65) | collective-permute-done | bytes 32800 | tf_op jit(solution)/shard_map/ppermute | solution.py:631
  46.7 1.2 %collective-permute-start.66 = (f32[8,1024]{1,0:T(8,128)S(1)}, f32[8,1024]{1,0:T(8,128)S(1)}, u32[]{:S(2)}, u32[]{:S(2)}) collective-permute-start(f32[8,1024]{1,0:T(8,128)S(1)} %add.9), channel_id=1, source_target_pairs={{0,1},{1,0},{2,3},{3,2},{4,5},{5,4},{6,7},{7,6},{8,9},{9,8},{10,11... | collective-permute-start | bytes 98312 | tf_op jit(solution)/shard_map/ppermute | solution.py:633
  47.9 0.9 %collective-permute-done.66 = f32[8,1024]{1,0:T(8,128)S(1)} collective-permute-done((f32[8,1024]{1,0:T(8,128)S(1)}, f32[8,1024]{1,0:T(8,128)S(1)}, u32[]{:S(2)}, u32[]{:S(2)}) %collective-permute-start.66) | collective-permute-done | bytes 32800 | tf_op jit(solution)/shard_map/ppermute | solution.py:633
  48.7 2.3 %collective-permute-start.67 = (f32[8,1024]{1,0:T(8,128)S(1)}, f32[8,1024]{1,0:T(8,128)S(1)}, u32[]{:S(2)}, u32[]{:S(2)}) collective-permute-start(f32[8,1024]{1,0:T(8,128)S(1)} %add.10), channel_id=1, source_target_pairs={{0,4},{4,0},{8,12},{12,8},{1,5},{5,1},{9,13},{13,9},{2,6},{6,2},{1... | collective-permute-start | bytes 98312 | tf_op jit(solution)/shard_map/ppermute | solution.py:637
  51.0 1.9 %collective-permute-done.67 = f32[8,1024]{1,0:T(8,128)S(1)} collective-permute-done((f32[8,1024]{1,0:T(8,128)S(1)}, f32[8,1024]{1,0:T(8,128)S(1)}, u32[]{:S(2)}, u32[]{:S(2)}) %collective-permute-start.67) | collective-permute-done | bytes 32800 | tf_op jit(solution)/shard_map/ppermute | solution.py:637
  52.9 4.1 %collective-permute-start.68 = (f32[8,1024]{1,0:T(8,128)S(1)}, f32[8,1024]{1,0:T(8,128)S(1)}, u32[]{:S(2)}, u32[]{:S(2)}) collective-permute-start(f32[8,1024]{1,0:T(8,128)S(1)} %add.11.sums_ref), channel_id=1, source_target_pairs={{0,8},{4,12},{8,0},{12,4},{1,9},{5,13},{9,1},{13,5},{2,10},{6,14},... | collective-permute-start | bytes 98312 | tf_op jit(solution)/shard_map/ppermute | solution.py:637
  57.0 1.9 %shard_map.140.y_ref = f32[512,384]{1,0:T(8,128)S(1)} custom-call(bf16[512,768]{1,0:T(8,128)(2,1)} %x_ref.1, bf16[4,512,128]{2,1,0:T(8,128)(2,1)S(1)} %get-tuple-element.273.out_ref, bf16[512,768]{1,0:T(8,128)(2,1)S(1)} %get-tuple-element.274.wide_ref), custom_call_target="tpu_custom_call" | custom-call | flops 1000000000 | bytes 4000000 | tf_op jit(solution)/shard_map/pallas_call | solution.py:640
  59.6 0.0 collective-permute-done.68.other_ref
  59.6 1.8 %shard_map.143 = (f32[8,256]{1,0:T(8,128)}, f32[8]{0:T(128)}) custom-call(s32[8]{0:T(128)S(1)} %copy-done.18, s32[8]{0:T(128)S(1)} %copy-done, f32[1]{0:T(128)S(6)} %copy.47.scale_ref, f32[8,1024]{1,0:T(8,128)S(1)} %add.11.sums_ref, f32[8,1024]{1,0:T(8,128)S(1)} %collective-permute-done.68.other_ref, bf16[256,384]{1,0:T(8,128)(2,1)S(1)} %copy-done.10, ...), custom_call_target="tpu_custom_call" | custom-call | flops 1000000 | bytes 1000000 | tf_op jit(solution)/shard_map/pallas_call | solution.py:668
  61.4 0.0 collective-permute-done.64.got_ref
  61.4 1.2 %shard_map.142 = bf16[512,384]{1,0:T(8,128)(2,1)} custom-call(f32[512,384]{1,0:T(8,128)S(1)} %shard_map.140.y_ref, bf16[512,384]{1,0:T(8,128)(2,1)S(1)} %collective-permute-done.64.got_ref), custom_call_target="tpu_custom_call" | custom-call | flops 100000000 | bytes 2000000 | tf_op jit(solution)/shard_map/pallas_call | solution.py:649
  (9 shorter events, 0.1 us)
Async XLA Ops:
  0.6 5.1 %copy-start.1 = (bf16[768,3,384]{2,0,1:T(8,128)(2,1)S(1)}, bf16[768,3,384]{2,0,1:T(8,128)(2,1)}, u32[]{:S(2)}) copy-start(bf16[768,3,384]{2,0,1:T(8,128)(2,1)} %param.22) | copy-start | bytes 5308420
  0.6 5.1 %copy-start.2 = (bf16[512,768]{1,0:T(8,128)(2,1)S(1)}, bf16[512,768]{1,0:T(8,128)(2,1)}, u32[]{:S(2)}) copy-start(bf16[512,768]{1,0:T(8,128)(2,1)} %x_ref.1) | copy-start | bytes 2359300
  0.7 5.1 %copy-start.18 = (s32[8]{0:T(128)S(1)}, s32[8]{0:T(128)}, u32[]{:S(2)}) copy-start(s32[8]{0:T(128)} %len_ref.3) | copy-start | bytes 100
  0.7 5.1 %copy-start.19 = (f32[384]{0:T(512)S(1)}, f32[384]{0:T(512)}, u32[]{:S(2)}) copy-start(f32[384]{0:T(512)} %param.23) | copy-start | bytes 4612
  5.8 14.5 %copy-start.11 = (bf16[256,384]{1,0:T(8,128)(2,1)S(1)}, bf16[256,384]{1,0:T(8,128)(2,1)}, u32[]{:S(2)}) copy-start(bf16[256,384]{1,0:T(8,128)(2,1)} %get-tuple-element.151.rep_ref) | copy-start | bytes 589828 | tf_op jit(solution)/shard_map/cond
  5.8 16.6 %copy-start.3 = (bf16[384,768]{1,0:T(8,128)(2,1)S(1)}, bf16[384,768]{1,0:T(8,128)(2,1)}, u32[]{:S(2)}) copy-start(bf16[384,768]{1,0:T(8,128)(2,1)} %get-tuple-element.150.w_out_ref) | copy-start | bytes 1769476 | tf_op jit(solution)/shard_map/cond
  5.9 20.4 %collective-permute-start = (bf16[3072,128]{1,0:T(8,128)(2,1)S(1)}, bf16[3072,128]{1,0:T(8,128)(2,1)S(1)}, u32[]{:S(2)}, u32[]{:S(2)}) collective-permute-start(bf16[3072,128]{1,0:T(8,128)(2,1)S(1)} %slice.27), channel_id=1, source_target_pairs={{0,1},{1,0},{2,3},{3,2},{4,5},{5,4},{6,7},{7,6},{8,9},{9,8},{10,11... | collective-permute-start | bytes 2359304 | tf_op jit(solution)/shard_map/cond/branch_0_fun/ppermute | solution.py:566
  6.5 13.8 %collective-permute-start.1 = (bf16[1216,128]{1,0:T(8,128)(2,1)S(1)}, bf16[1216,128]{1,0:T(8,128)(2,1)S(1)}, u32[]{:S(2)}, u32[]{:S(2)}) collective-permute-start(bf16[1216,128]{1,0:T(8,128)(2,1)S(1)} %slice.33), channel_id=1, source_target_pairs={{0,4},{4,0},{8,12},{12,8},{1,5},{5,1},{9,13},{13,9},{2,6},{6,2},{1... | collective-permute-start | bytes 933896 | tf_op jit(solution)/shard_map/cond/branch_0_fun/ppermute | solution.py:565
  9.2 12.7 %collective-permute-start.3 = (bf16[576,128]{1,0:T(8,128)(2,1)S(1)}, bf16[576,128]{1,0:T(8,128)(2,1)S(1)}, u32[]{:S(2)}, u32[]{:S(2)}) collective-permute-start(bf16[576,128]{1,0:T(8,128)(2,1)S(1)} %slice.44), channel_id=1, source_target_pairs={{0,8},{4,12},{8,0},{12,4},{1,9},{5,13},{9,1},{13,5},{2,10},{6,14},... | collective-permute-start | bytes 442376 | tf_op jit(solution)/shard_map/cond/branch_0_fun/ppermute | solution.py:565
  11.8 10.3 %collective-permute-start.5 = (bf16[576,128]{1,0:T(8,128)(2,1)S(1)}, bf16[576,128]{1,0:T(8,128)(2,1)S(1)}, u32[]{:S(2)}, u32[]{:S(2)}) collective-permute-start(bf16[576,128]{1,0:T(8,128)(2,1)S(1)} %slice.44), channel_id=1, source_target_pairs={{4,8},{8,4},{5,9},{9,5},{6,10},{10,6},{7,11},{11,7},{20,24},{24,20... | collective-permute-start | bytes 442376 | tf_op jit(solution)/shard_map/cond/branch_0_fun/ppermute | solution.py:565
  20.3 11.9 %collective-permute-start.2 = (bf16[1216,128]{1,0:T(8,128)(2,1)S(1)}, bf16[1216,128]{1,0:T(8,128)(2,1)S(1)}, u32[]{:S(2)}, u32[]{:S(2)}) collective-permute-start(bf16[1216,128]{1,0:T(8,128)(2,1)S(1)} %collective-permute-done.1.rest_2_), channel_id=1, source_target_pairs={{0,1},{1,0},{2,3},{3,2},{4,5},{5,4},{6,7},{7,6},{8,9},{9,8},{10,11... | collective-permute-start | bytes 933896 | tf_op jit(solution)/shard_map/cond/branch_0_fun/ppermute | solution.py:603
  20.3 12.8 %collective-permute-start.7 = (bf16[256,384]{1,0:T(8,128)(2,1)S(1)}, bf16[256,384]{1,0:T(8,128)(2,1)}, u32[]{:S(2)}, u32[]{:S(2)}) collective-permute-start(bf16[256,384]{1,0:T(8,128)(2,1)S(1)} %copy-done.11), channel_id=1, source_target_pairs={{0,2},{2,0},{1,3},{3,1},{4,6},{6,4},{5,7},{7,5},{8,10},{10,8},{9,1... | collective-permute-start | bytes 589832 | tf_op jit(solution)/shard_map/cond/branch_0_fun/ppermute | solution.py:568
  21.9 10.3 %collective-permute-start.4 = (bf16[576,128]{1,0:T(8,128)(2,1)S(1)}, bf16[576,128]{1,0:T(8,128)(2,1)S(1)}, u32[]{:S(2)}, u32[]{:S(2)}) collective-permute-start(bf16[576,128]{1,0:T(8,128)(2,1)S(1)} %collective-permute-done.3.rest_4_), channel_id=1, source_target_pairs={{0,1},{1,0},{2,3},{3,2},{4,5},{5,4},{6,7},{7,6},{8,9},{9,8},{10,11... | collective-permute-start | bytes 442376 | tf_op jit(solution)/shard_map/cond/branch_0_fun/ppermute | solution.py:603
  22.1 10.1 %collective-permute-start.6 = (bf16[576,128]{1,0:T(8,128)(2,1)S(1)}, bf16[576,128]{1,0:T(8,128)(2,1)S(1)}, u32[]{:S(2)}, u32[]{:S(2)}) collective-permute-start(bf16[576,128]{1,0:T(8,128)(2,1)S(1)} %collective-permute-done.5.rest_6_), channel_id=1, source_target_pairs={{0,1},{1,0},{2,3},{3,2},{4,5},{5,4},{6,7},{7,6},{8,9},{9,8},{10,11... | collective-permute-start | bytes 442376 | tf_op jit(solution)/shard_map/cond/branch_0_fun/ppermute | solution.py:603
  35.3 24.3 %copy-start = (s32[8]{0:T(128)S(1)}, s32[8]{0:T(128)}, u32[]{:S(2)}) copy-start(s32[8]{0:T(128)} %pairs_ref.1) | copy-start | bytes 100
  35.3 24.3 %copy-start.10 = (bf16[256,384]{1,0:T(8,128)(2,1)S(1)}, bf16[256,384]{1,0:T(8,128)(2,1)}, u32[]{:S(2)}) copy-start(bf16[256,384]{1,0:T(8,128)(2,1)} %rest_0_.1) | copy-start | bytes 589828
  35.3 26.1 %collective-permute-start.64 = (bf16[512,384]{1,0:T(8,128)(2,1)S(1)}, bf16[512,384]{1,0:T(8,128)(2,1)S(1)}, u32[]{:S(2)}, u32[]{:S(2)}) collective-permute-start(bf16[512,384]{1,0:T(8,128)(2,1)S(1)} %get-tuple-element.276), channel_id=1, source_target_pairs={{0,2},{2,0},{1,3},{3,1},{4,6},{6,4},{5,7},{7,5},{8,10},{10,8},{9,1... | collective-permute-start | bytes 1179656 | tf_op jit(solution)/shard_map/ppermute | solution.py:632
  35.4 11.3 %collective-permute-start.65 = (f32[8,1024]{1,0:T(8,128)S(1)}, f32[8,1024]{1,0:T(8,128)S(1)}, u32[]{:S(2)}, u32[]{:S(2)}) collective-permute-start(f32[8,1024]{1,0:T(8,128)S(1)} %get-tuple-element.277), channel_id=1, source_target_pairs={{0,2},{2,0},{1,3},{3,1},{4,6},{6,4},{5,7},{7,5},{8,10},{10,8},{9,1... | collective-permute-start | bytes 98312 | tf_op jit(solution)/shard_map/ppermute | solution.py:631
  46.7 2.0 %collective-permute-start.66 = (f32[8,1024]{1,0:T(8,128)S(1)}, f32[8,1024]{1,0:T(8,128)S(1)}, u32[]{:S(2)}, u32[]{:S(2)}) collective-permute-start(f32[8,1024]{1,0:T(8,128)S(1)} %add.9), channel_id=1, source_target_pairs={{0,1},{1,0},{2,3},{3,2},{4,5},{5,4},{6,7},{7,6},{8,9},{9,8},{10,11... | collective-permute-start | bytes 98312 | tf_op jit(solution)/shard_map/ppermute | solution.py:633
  48.7 4.2 %collective-permute-start.67 = (f32[8,1024]{1,0:T(8,128)S(1)}, f32[8,1024]{1,0:T(8,128)S(1)}, u32[]{:S(2)}, u32[]{:S(2)}) collective-permute-start(f32[8,1024]{1,0:T(8,128)S(1)} %add.10), channel_id=1, source_target_pairs={{0,4},{4,0},{8,12},{12,8},{1,5},{5,1},{9,13},{13,9},{2,6},{6,2},{1... | collective-permute-start | bytes 98312 | tf_op jit(solution)/shard_map/ppermute | solution.py:637
  52.9 6.7 %collective-permute-start.68 = (f32[8,1024]{1,0:T(8,128)S(1)}, f32[8,1024]{1,0:T(8,128)S(1)}, u32[]{:S(2)}, u32[]{:S(2)}) collective-permute-start(f32[8,1024]{1,0:T(8,128)S(1)} %add.11.sums_ref), channel_id=1, source_target_pairs={{0,8},{4,12},{8,0},{12,4},{1,9},{5,13},{9,1},{13,5},{2,10},{6,14},... | collective-permute-start | bytes 98312 | tf_op jit(solution)/shard_map/ppermute | solution.py:637
